TPU v7x, 256 devices: a whole 4x4x8 slice. The times are simulated.
256 devices in a mesh: seq: 32 (over y, z_lo, core), head: 8 (over x, z_hi).
Axes of the slice: x: 4, y: 4, z: 8 (z_hi: 2, z_lo: 4; z = z_hi * 4 + z_lo), core: 2. Of those that a mesh axis runs over, the one named last changes fastest.
Arguments:
- queries: bfloat16 [4096, 16384], P('seq', 'head'), may hold values from -16 to 16
- keys: bfloat16 [4096, 1024], P('seq', 'head'), may hold values from -12 to 12
- values: bfloat16 [4096, 1024], P('seq', 'head'), may hold values from -6 to 6
- feat_q: bfloat16 [128, 128, 128], P('head'), may hold values from -0.6 to 0.6
- feat_k: bfloat16 [128, 128, 128], P('head'), may hold values from -0.6 to 0.6
Outputs:
- student: bfloat16 [4096, 16384], P('seq', 'head')
- token_loss: float32 [4096], P(('seq', 'head'))
All inputs are finite; a program needn't handle non-finite values.
Results may differ from a plain program's by a relative error of at most 0.0035.
Values may be sent and summed in bfloat16 or wider, within the bound.
No kernel may reach another device: no remote copies, remote signals or barrier semaphores. Data moves between devices by JAX's collectives and lax.ppermute only.
A program may use at most 128 MiB of HBM per device.

v0:
```python
import math

import jax
import jax.numpy as jnp
from jax import lax
from jax.experimental import pallas as pl
from jax.experimental.pallas import tpu as pltpu
from jax.sharding import Mesh
from jax.sharding import PartitionSpec as P


HQ = 128
D = 128
F = 2 * D
LOG2E = math.log2(math.e)
SCALE = LOG2E / math.sqrt(D)
NEG = -1e30
SEQ = ("y", "z", "c")
F32, BF16 = jnp.float32, jnp.bfloat16
VMEM = pl.BlockSpec(memory_space=pltpu.VMEM)
SMEM = pl.BlockSpec(memory_space=pltpu.SMEM)
ANY = pl.BlockSpec(memory_space=pl.ANY)
HBM = pl.BlockSpec(memory_space=pltpu.HBM)


def mm(a, b):
    return jnp.dot(a, b, preferred_element_type=F32)


def mm_t(a, b):
    return lax.dot_general(a, b, (((1,), (1,)), ((), ())), preferred_element_type=F32)


def split(x):
    high = x.astype(BF16)
    return high, (x - high.astype(F32)).astype(BF16)


def both_softmax(x, axis):
    up = jnp.exp2(x - jnp.max(x, axis, keepdims=True))
    down = jnp.exp2(jnp.min(x, axis, keepdims=True) - x)
    up = up * (1.0 / jnp.sum(up, axis, keepdims=True))
    down = down * (1.0 / jnp.sum(down, axis, keepdims=True))
    return up.astype(BF16), down.astype(BF16)


def fill(k2_ref, v1_ref, at, kv):
    rows = kv.shape[0]
    k2_ref[at : at + rows, :D] = kv[:, :D]
    k2_ref[at : at + rows, D:] = kv[:, :D]
    v1_ref[at : at + rows, :D] = kv[:, D:]
    v1_ref[at : at + rows, D:] = jnp.ones((rows, D), BF16)


def prepare(q_ref, fq_ref, fk_ref, q2_ref, qf_ref, wk_ref, wk_later_ref):
    tokens = q_ref.shape[0]

    def head(h, _):
        q = q_ref[:, pl.ds(pl.multiple_of(h * D, D), D)]
        rows = pl.ds(pl.multiple_of(h * tokens, tokens), tokens)
        high, low = split(q.astype(F32) * SCALE)
        q2_ref[rows, :D] = high
        q2_ref[rows, D:] = low
        up, down = both_softmax(mm(q, fq_ref[h]) * LOG2E, 1)
        qf_ref[rows, :D] = up
        qf_ref[rows, D:] = down
        high, low = split((fk_ref[h].astype(F32) * LOG2E).T)
        rows = pl.ds(pl.multiple_of(h * D, D), D)
        for ref in (wk_ref, wk_later_ref):
            ref[rows, :D] = high
            ref[rows, D:] = low
        return 0

    lax.fori_loop(0, fq_ref.shape[0], head, 0, unroll=4)


def lane_blocks(s):
    return [s[:, i : i + D] for i in range(0, s.shape[1], D)]


def row_max(parts):
    while len(parts) > 1:
        parts = [jnp.maximum(a, b) for a, b in zip(parts[::2], parts[1::2])]
    return jnp.max(parts[0], 1, keepdims=True)


def own_row(at_ref, q2_ref, qf_ref, wk_ref, mine_ref, other_ref, acc_ref, m_ref, near_ref, k2, v1, bias, keep, s0, s1, x0, x1, f0, f1, p0, p1, a0, a1):
    tokens = keep.shape[0]
    heads = qf_ref.shape[0] // tokens
    half = mine_ref.shape[0]
    wide = k2.shape[0]
    many = s0.shape[0] // tokens
    groups = heads // many
    tile = wide // many
    z, c = at_ref[1], at_ref[2]
    safe = jnp.broadcast_to(mine_ref[:16, :D].astype(F32)[:1], (tokens, D))
    for side, ref in enumerate((mine_ref, other_ref)):
        for slot in range(half // tokens):
            kv = ref[slot * tokens : (slot + 1) * tokens].astype(F32)
            key, value, one = kv[:, :D], kv[:, D:], jnp.ones((tokens, D), F32)
            if slot or side:
                seen = slot <= z if slot else c == 1
                key = jnp.where(seen, key, safe)
                value = jnp.where(seen, value, 0.0)
                one = jnp.where(seen, one, 0.0)
            here = slice(side * half + slot * tokens, side * half + (slot + 1) * tokens)
            k2[here, :D] = key.astype(BF16)
            k2[here, D:] = key.astype(BF16)
            v1[here, :D] = value.astype(BF16)
            v1[here, D:] = one.astype(BF16)
    row = lax.broadcasted_iota(jnp.int32, (tokens, tokens), 0)
    col = lax.broadcasted_iota(jnp.int32, (tokens, tokens), 1)
    seen = (col <= row).astype(F32)
    keep[...] = seen
    bias[...] = (1.0 - seen) * NEG

    def block(g, size):
        return pl.ds(pl.multiple_of(g * size, size), size)

    def first(g, s, x, j):
        cols = slice(j * tile, (j + 1) * tile)
        s[:, cols] = mm_t(q2_ref[block(g, many * tokens)], k2[cols])
        x[:, cols] = mm_t(wk_ref[block(g, many * D)], k2[cols])

    def second(g, s, x, p, f, i):
        here = slice(i * tokens, (i + 1) * tokens)
        parts = lane_blocks(s[here])
        parts[0] = parts[0] + bias[...]
        m = row_max(parts)
        m_ref[block(g * many + i, tokens)] = jnp.broadcast_to(m, (tokens, D))
        p[here] = jnp.concatenate([jnp.exp2(a - m).astype(BF16) for a in parts], 1)
        up, down = both_softmax(x[i * D : (i + 1) * D], 0)
        f[i * F : i * F + D] = up
        f[i * F + D : (i + 1) * F] = down

    def third(g, f, a, i):
        here = slice(i * tokens, (i + 1) * tokens)
        scores = mm(qf_ref[block(g * many + i, tokens)], f[i * F : (i + 1) * F])
        a[here, :D] = (scores[:, :D] * keep[...]).astype(BF16)
        a[here, D:] = scores[:, D:].astype(BF16)

    def mix(out_ref, g, p):
        out_ref[block(g, many * tokens)] = mm(p[...], v1[...])

    def stage(g, s, x, p, f, s_next, x_next, p_last, f_last, a_last, a_older):
        last, older = jnp.maximum(g - 1, 0), jnp.maximum(g - 2, 0)
        for j in range(many):
            first(jnp.minimum(g + 1, groups - 1), s_next, x_next, j)
            second(g, s, x, p, f, j)
            third(last, f_last, a_last, j)
            if j == 0:
                mix(acc_ref, last, p_last)
            if j == 2:
                mix(near_ref, older, a_older)

    for j in range(many):
        first(0, s0, x0, j)
    f1[...] = jnp.zeros_like(f1)
    p1[...] = jnp.zeros_like(p1)
    a0[...] = jnp.zeros_like(a0)

    def step(i, _):
        g = 2 * i
        stage(g, s0, x0, p0, f0, s1, x1, p1, f1, a1, a0)
        stage(g + 1, s1, x1, p1, f1, s0, x0, p0, f0, a0, a1)
        return 0

    lax.fori_loop(0, groups // 2, step, 0)
    mix(acc_ref, groups - 1, p1)
    mix(near_ref, groups - 2, a0)
    for j in range(many):
        third(groups - 1, f1, a1, j)
    mix(near_ref, groups - 1, a1)


def earlier_state(at_ref, wk_ref, *refs):
    rows, (out_ref, k2, v1, state, x0, x1, f0, f1) = refs[:-8], refs[-8:]
    heads = out_ref.shape[0] // F
    half = rows[0].shape[0]
    pairs = heads // 2
    count = at_ref[0] * pairs
    state[...] = jnp.zeros_like(state)
    f1[...] = jnp.zeros_like(f1)
    for k, row_ref in enumerate(rows):

        @pl.when(at_ref[0] > k)
        def _(k=k, row_ref=row_ref):
            fill(k2, v1, k * half, row_ref[...])

    def place(t):
        t = jnp.clip(t, 0, jnp.maximum(count - 1, 0))
        k, pair = lax.div(t, pairs), lax.rem(t, pairs)
        return pl.ds(pl.multiple_of(k * half, half), half), pair

    def first(t, x):
        at, pair = place(t)
        x[...] = mm_t(wk_ref[pl.ds(pl.multiple_of(pair * 2 * D, 2 * D), 2 * D)], k2[at])

    def second(x, f):
        for i in range(2):
            up, down = both_softmax(x[i * D : (i + 1) * D], 0)
            f[i * F : i * F + D] = up
            f[i * F + D : (i + 1) * F] = down

    def third(t, f):
        at, pair = place(t)
        state[pl.ds(pl.multiple_of(pair * 2 * F, 2 * F), 2 * F)] += mm(f[...], v1[at])

    @pl.when(count > 0)
    def _():
        first(0, x0)

        def step(i, _):
            t = 2 * i
            first(t + 1, x1)
            second(x0, f0)
            third(t - 1, f1)
            first(t + 2, x0)
            second(x1, f1)
            third(t, f0)
            return 0

        lax.fori_loop(0, lax.div(count, 2), step, 0)
        third(count - 1, f1)

    out_ref[...] = state[...].astype(BF16)


def earlier_teacher(at_ref, q2_ref, acc0_ref, m0_ref, *refs):
    rows, (acc, k2, v1, m_all, s0, s1, p0, p1) = refs[:-8], refs[-8:]
    half = rows[0].shape[0]
    wide = 2 * half
    part = s0.shape[0]
    groups = q2_ref.shape[0] // part
    count = at_ref[0] * groups
    m_all[...] = m0_ref[...]
    for k in range(len(rows) // 2):

        @pl.when(at_ref[0] > k)
        def _(k=k):
            fill(k2, v1, k * wide, rows[2 * k][...])
            fill(k2, v1, k * wide + half, rows[2 * k + 1][...])

    def place(t):
        t = jnp.clip(t, 0, jnp.maximum(count - 1, 0))
        k, g = lax.div(t, groups), lax.rem(t, groups)
        return pl.ds(pl.multiple_of(k * wide, wide), wide), pl.multiple_of(g * part, part)

    def first(t, s):
        at, g = place(t)
        s[...] = mm_t(q2_ref[pl.ds(g, part)], k2[at])

    def second(t, s, p):
        _, g = place(t)
        for i in range(0, part, D):
            here = pl.ds(pl.multiple_of(g + i, D), D)
            before = m_all[here]
            m = jnp.maximum(before, row_max(lane_blocks(s[i : i + D])))
            m_all[here] = m
            factor = jnp.exp2(before - m)
            acc[here] = acc[here] * jnp.concatenate([factor, factor], 1)
            m = jnp.concatenate([m] * (wide // D), 1)
            p[i : i + D] = jnp.exp2(s[i : i + D] - m).astype(BF16)

    def third(t, p):
        at, g = place(t)
        acc[pl.ds(g, part)] += mm(p[...], v1[at])

    @pl.when(count > 0)
    def _():
        first(0, s0)

        def step(i, _):
            t = 2 * i
            first(t + 1, s1)
            second(t, s0, p0)
            third(t, p0)
            first(t + 2, s0)
            second(t + 1, s1, p1)
            third(t + 1, p1)
            return 0

        lax.fori_loop(0, lax.div(count, 2), step, 0)


def finish(qf_ref, near_ref, mine_ref, other_ref, acc_ref, student_ref, loss_ref, total, out, sems):
    tokens = total.shape[0]
    heads = qf_ref.shape[0] // tokens
    many = heads // sems.shape[0]
    total[...] = jnp.zeros_like(total)
    copies = []
    for h in range(heads):
        here = slice(h * tokens, (h + 1) * tokens)
        there = slice(h * F, (h + 1) * F)
        qf = qf_ref[here]
        sums = near_ref[here] + mm(qf, mine_ref[there]) + mm(qf, other_ref[there])
        student = sums[:, :D] * (1.0 / sums[:, D:])
        out[:, h * D : (h + 1) * D] = student.astype(BF16)
        acc = acc_ref[here]
        total[...] += (student - acc[:, :D] * (1.0 / acc[:, D:])) ** 2
        if (h + 1) % many == 0:
            i = h // many
            cols = slice(i * many * D, (i + 1) * many * D)
            copies.append(pltpu.make_async_copy(out.at[:, cols], student_ref.at[:, cols], sems.at[i]))
            copies[-1].start()
    per_token = jnp.sum(total[...].T, 0, keepdims=True) * (1.0 / HQ)
    blocks, width = loss_ref.shape
    t = lax.broadcasted_iota(jnp.int32, (blocks, tokens), 1)
    b = lax.broadcasted_iota(jnp.int32, (blocks, tokens), 0)
    own = (t >= b * width) & (t < (b + 1) * width)
    ti = lax.broadcasted_iota(jnp.int32, (tokens, width), 0)
    ji = lax.broadcasted_iota(jnp.int32, (tokens, width), 1)
    pick = jnp.zeros((tokens, width), F32)
    for i in range(blocks):
        pick = pick + (ti == ji + i * width).astype(F32)
    loss_ref[...] = jnp.dot(
        jnp.where(own, jnp.broadcast_to(per_token, (blocks, tokens)), 0.0),
        pick,
        precision=lax.Precision.HIGHEST,
        preferred_element_type=F32,
    )
    for copy in copies:
        copy.wait()


def pack(keys_ref, values_ref, kv_ref, sems):
    copies = [
        pltpu.make_async_copy(src, kv_ref.at[:, i * D : (i + 1) * D], sems.at[i])
        for i, src in enumerate((keys_ref, values_ref))
    ]
    for copy in copies:
        copy.start()
    for copy in copies:
        copy.wait()


def call(kernel, outs, scratch, us, mib, *args, scalars=0, aliases=None, ins=None, spec=None):
    return pl.pallas_call(
        kernel,
        out_shape=outs,
        in_specs=ins or [SMEM] * scalars + [VMEM] * (len(args) - scalars),
        out_specs=spec or jax.tree.map(lambda _: VMEM, outs),
        scratch_shapes=scratch,
        input_output_aliases=aliases or {},
        cost_estimate=pl.CostEstimate(
            flops=int(us * 1e9), bytes_accessed=1 << 20, transcendentals=0
        ),
        compiler_params=pltpu.CompilerParams(vmem_limit_bytes=mib << 20),
    )(*args)


def shape(dims, dtype=F32):
    return jax.ShapeDtypeStruct(dims, dtype)


def shifted(x, axis, k):
    n = lax.axis_size(axis)
    return lax.ppermute(x, axis, [(i, (i + k) % n) for i in range(n)])


def body(queries, keys, values, feat_q, feat_k):
    tokens = queries.shape[0]
    heads = feat_q.shape[0]
    depth = lax.axis_size("y")
    at = jnp.stack([lax.axis_index(a) for a in SEQ]).astype(jnp.int32)
    rows = heads * tokens
    kv = call(
        pack,
        shape((tokens, F), BF16),
        [pltpu.SemaphoreType.DMA((2,))],
        1,
        1,
        keys,
        values,
        ins=[HBM, HBM],
    )
    zs = [shifted(kv, "z", k) for k in range(1, lax.axis_size("z"))]
    q2, qf, wk, wk_later = call(
        prepare,
        (shape((rows, F), BF16),) * 2 + (shape((heads * D, F), BF16),) * 2,
        [],
        3,
        10,
        queries,
        feat_q,
        feat_k,
    )
    zs, q2, qf, wk = lax.optimization_barrier((zs, q2, qf, wk))
    row = jnp.concatenate([kv, *zs], 0)
    half = row.shape[0]
    above = [shifted(row, "y", k) for k in range(1, depth)]
    other = shifted(row, "c", 1)
    many = 4
    acc0, m0, near = call(
        own_row,
        (shape((rows, F)), shape((rows, D)), shape((rows, F))),
        [pltpu.VMEM((2 * half, F), BF16)] * 2
        + [pltpu.VMEM((tokens, tokens), F32)] * 2
        + [pltpu.VMEM((many * tokens, 2 * half), F32)] * 4
        + [pltpu.VMEM((many * F, 2 * half), BF16)] * 2
        + [pltpu.VMEM((many * tokens, 2 * half), BF16)] * 4,
        10,
        30,
        at,
        q2,
        qf,
        wk,
        row,
        other,
        scalars=1,
    )
    above, acc0, m0, near = lax.optimization_barrier((above, acc0, m0, near))
    above_other = []
    for a in above:
        above_other.append(shifted(a, "c", 1))
    earlier = (depth - 1) * half
    state = call(
        earlier_state,
        shape((heads * F, F), BF16),
        [pltpu.VMEM((earlier, F), BF16)] * 2
        + [pltpu.VMEM((heads * F, F), F32)]
        + [pltpu.VMEM((2 * D, half), F32)] * 2
        + [pltpu.VMEM((2 * F, half), BF16)] * 2,
        5,
        14,
        at,
        wk_later,
        *above,
        scalars=1,
    )
    state_other = shifted(state, "c", 1)
    pairs = [r for pair in zip(above, above_other) for r in pair]
    acc = call(
        earlier_teacher,
        shape((rows, F)),
        [pltpu.VMEM((2 * earlier, F), BF16)] * 2
        + [pltpu.VMEM((rows, D), F32)]
        + [pltpu.VMEM((many * tokens, 2 * half), F32)] * 2
        + [pltpu.VMEM((many * tokens, 2 * half), BF16)] * 2,
        8,
        18,
        at,
        q2,
        acc0,
        m0,
        *pairs,
        scalars=1,
        aliases={2: 0},
    )
    parts = lax.axis_size("head")
    student, loss = call(
        finish,
        (shape((tokens, heads * D), BF16), shape((parts, tokens // parts))),
        [
            pltpu.VMEM((tokens, D), F32),
            pltpu.VMEM((tokens, heads * D), BF16),
            pltpu.SemaphoreType.DMA((4,)),
        ],
        2,
        14,
        qf,
        near,
        state,
        state_other,
        acc,
        spec=(ANY, VMEM),
    )
    tiles = lax.all_to_all(loss[:, None, :], "head", 0, 0, tiled=True)
    return student, jnp.sum(tiles, axis=(0, 1))


def solution(mesh):
    grid = Mesh(mesh.devices.reshape(4, 4, 2, mesh.shape["head"]), (*SEQ, "head"))
    placed = P(SEQ, "head")
    return jax.shard_map(
        body,
        mesh=grid,
        in_specs=(placed, placed, placed, P("head"), P("head")),
        out_specs=(placed, P((*SEQ, "head"))),
        check_vma=False,
    )
```

profile of v0, /device:TPU:24, one launch (start us, length us, event | category | flops | bytes accessed | tf_op | source)
XLA Modules:
  0.0 79.6 jit_solution(2133075621530633631)
XLA Ops:
  0.7 0.8 %copy-done.3 = bf16[128,128]{1,0:T(8,128)(2,1)S(1)} copy-done((bf16[128,128]{1,0:T(8,128)(2,1)S(1)}, bf16[128,128]{1,0:T(8,128)(2,1)}, u32[]{:S(2)}) %copy-start.3) | copy-done | bytes 32792
  1.5 0.8 copy-done.4
  2.3 4.7 %collective-permute-start.2 = (bf16[128,256]{1,0:T(8,128)(2,1)S(1)}, bf16[128,256]{1,0:T(8,128)(2,1)S(1)}, u32[]{:S(2)}, u32[]{:S(2)}) collective-permute-start(bf16[128,256]{1,0:T(8,128)(2,1)S(1)} %shard_map.68), channel_id=1, source_target_pairs={{0,48},{16,0},{32,16},{48,32},{1,49},{17,1},{33,17},{49,33},{2,50}... | collective-permute-start | bytes 196616 | tf_op jit(solution)/shard_map/ppermute | solution.py:358
  7.0 0.7 collective-permute-start
  7.7 3.2 %shard_map.69 = (bf16[2048,256]{1,0:T(8,128)(2,1)S(1)}, bf16[2048,256]{1,0:T(8,128)(2,1)S(1)}, bf16[2048,256]{1,0:T(8,128)(2,1)S(1)}, bf16[2048,256]{1,0:T(8,128)(2,1)S(1)}) custom-call(bf16[128,2048]{1,0:T(8,128)(2,1)S(1)} %copy-done, bf16[16,128,128]{2,1,0:T(8,128)(2,1)S(1)} %copy-done.1, bf16[16,128,128]{2,1,0:T(8,128)(2,1)S(1)} %copy-done.2), custom_call_target="tpu_custom_call" | custom-call | flops 3000000000 | bytes 1048576 | tf_op jit(solution)/shard_map/pallas_call | solution.py:338
  10.9 1.0 %copy-done.5 = bf16[2048,256]{1,0:T(8,128)(2,1)} copy-done((bf16[2048,256]{1,0:T(8,128)(2,1)}, bf16[2048,256]{1,0:T(8,128)(2,1)S(1)}, u32[]{:S(2)}) %copy-start.5) | copy-done | bytes 1048600
  11.9 1.0 %copy-done.7 = bf16[2048,256]{1,0:T(8,128)(2,1)} copy-done((bf16[2048,256]{1,0:T(8,128)(2,1)}, bf16[2048,256]{1,0:T(8,128)(2,1)S(1)}, u32[]{:S(2)}) %copy-start.7) | copy-done | bytes 1048600
  12.9 0.4 collective-permute-done.1
  13.5 0.8 collective-permute-start.5
  14.3 1.2 %collective-permute-start.4 = (bf16[512,256]{1,0:T(8,128)(2,1)S(1)}, bf16[512,256]{1,0:T(8,128)(2,1)S(1)}, u32[]{:S(2)}, u32[]{:S(2)}) collective-permute-start(bf16[512,256]{1,0:T(8,128)(2,1)S(1)} %pad_maximum_fusion.mine_ref), channel_id=1, source_target_pairs={{0,128},{64,192},{128,0},{192,64},{1,129},{65,193},{129,1},{193,65... | collective-permute-start | bytes 786440 | tf_op jit(solution)/shard_map/ppermute | solution.py:358
  15.4 2.0 %collective-permute-start.3 = (bf16[512,256]{1,0:T(8,128)(2,1)S(1)}, bf16[512,256]{1,0:T(8,128)(2,1)S(1)}, u32[]{:S(2)}, u32[]{:S(2)}) collective-permute-start(bf16[512,256]{1,0:T(8,128)(2,1)S(1)} %pad_maximum_fusion.mine_ref), channel_id=1, source_target_pairs={{0,64},{64,128},{128,192},{192,0},{1,65},{65,129},{129,193},{193,1... | collective-permute-start | bytes 786440 | tf_op jit(solution)/shard_map/ppermute | solution.py:358
  17.4 1.2 %copy-done.8 = bf16[2048,256]{1,0:T(8,128)(2,1)S(1)} copy-done((bf16[2048,256]{1,0:T(8,128)(2,1)S(1)}, bf16[2048,256]{1,0:T(8,128)(2,1)}, u32[]{:S(2)}) %copy-start.8) | copy-done | bytes 1048600
  18.6 12.1 %shard_map.70 = (f32[2048,256]{1,0:T(8,128)S(1)}, f32[2048,128]{1,0:T(8,128)S(1)}, f32[2048,256]{1,0:T(8,128)S(1)}) custom-call(s32[3]{0:T(128)S(1)} %pad_add_fusion.at_ref, bf16[2048,256]{1,0:T(8,128)(2,1)S(1)} %get-tuple-element.30.q2_ref, bf16[2048,256]{1,0:T(8,128)(2,1)S(1)} %get-tuple-element.26.qf_ref, bf16[2048,256]{1,0:T(8,128)(2,1)S(1)} %copy-done.8, ...), custom_call_target="tpu_custom_call" | custom-call | flops 10000000000 | bytes 1048576 | tf_op jit(solution)/shard_map/pallas_call | solution.py:338
  30.8 12.2 %shard_map.71.mine_ref = bf16[4096,256]{1,0:T(8,128)(2,1)S(1)} custom-call(s32[3]{0:T(128)S(1)} %pad_add_fusion.at_ref, bf16[2048,256]{1,0:T(8,128)(2,1)S(1)} %copy-done.6, bf16[512,256]{1,0:T(8,128)(2,1)S(1)} %collective-permute-done.3.refs_0_, bf16[512,256]{1,0:T(8,128)(2,1)S(1)} %collective-permute-done.4.refs_1_.refs_2_, ...), custom_call_target="tpu_custom_call" | custom-call | flops 5000000000 | bytes 1048576 | tf_op jit(solution)/shard_map/pallas_call | solution.py:338
  43.1 0.5 collective-permute-start.8
  43.6 0.1 collective-permute-start.9
  43.7 0.4 collective-permute-start.10
  44.1 3.5 %collective-permute-done.8.refs_1_ = bf16[512,256]{1,0:T(8,128)(2,1)S(1)} collective-permute-done((bf16[512,256]{1,0:T(8,128)(2,1)S(1)}, bf16[512,256]{1,0:T(8,128)(2,1)S(1)}, u32[]{:S(2)}, u32[]{:S(2)}) %collective-permute-start.8) | collective-permute-done | bytes 262176 | tf_op jit(solution)/shard_map/ppermute | solution.py:358
  47.6 0.4 collective-permute-done.9.refs_3_
  48.0 0.4 collective-permute-done.10.refs_5_
  48.4 10.3 %shard_map.72.acc_ref = f32[2048,256]{1,0:T(8,128)S(1)} custom-call(s32[3]{0:T(128)S(1)} %pad_add_fusion.at_ref, bf16[2048,256]{1,0:T(8,128)(2,1)S(1)} %get-tuple-element.30.q2_ref, f32[2048,256]{1,0:T(8,128)S(1)} %get-tuple-element.40.acc0_ref, f32[2048,128]{1,0:T(8,128)S(1)} %get-tuple-element.41.m0_ref, ...), custom_call_target="tpu_custom_call", output_to_operand_aliasing={{}: (2, {})} | custom-call | flops 8000000000 | bytes 1048576 | tf_op jit(solution)/shard_map/pallas_call | solution.py:338
  58.7 1.6 %shard_map.73 = (bf16[128,2048]{1,0:T(8,128)(2,1)}, f32[8,16]{1,0:T(8,128)S(1)}) custom-call(bf16[2048,256]{1,0:T(8,128)(2,1)S(1)} %get-tuple-element.26.qf_ref, f32[2048,256]{1,0:T(8,128)S(1)} %get-tuple-element.35.near_ref, bf16[4096,256]{1,0:T(8,128)(2,1)S(1)} %shard_map.71.mine_ref, bf16[4096,256]{1,0:T(8,128)(2,1)S(1)} %collective-permute-done.7.other_ref, ...), custom_call_target="tpu_custom_call" | custom-call | flops 2000000000 | bytes 1048576 | tf_op jit(solution)/shard_map/pallas_call | solution.py:338
  60.3 18.8 %all_to_all.5 = f32[8,1,16]{2,1,0:T(1,128)S(1)} all-to-all(f32[8,1,16]{2,1,0:T(1,128)S(1)} %bitcast.6), channel_id=1, replica_groups=mesh['y'=4,'z'=4,'c'=2,'head'=8] {'head'}, dimensions={0} | all-to-all | bytes 1024 | tf_op jit(solution)/shard_map/all_to_all | solution.py:468
  79.1 0.5 reduce_sum.9
  (26 shorter events, 0.4 us)
Async XLA Ops:
  0.6 7.0 %copy-start.2 = (bf16[16,128,128]{2,1,0:T(8,128)(2,1)S(1)}, bf16[16,128,128]{2,1,0:T(8,128)(2,1)}, u32[]{:S(2)}) copy-start(bf16[16,128,128]{2,1,0:T(8,128)(2,1)} %fk_ref.1) | copy-start | bytes 1572868
  0.6 7.0 %copy-start.1 = (bf16[16,128,128]{2,1,0:T(8,128)(2,1)S(1)}, bf16[16,128,128]{2,1,0:T(8,128)(2,1)}, u32[]{:S(2)}) copy-start(bf16[16,128,128]{2,1,0:T(8,128)(2,1)} %fq_ref.1) | copy-start | bytes 1572868
  0.7 0.8 %copy-start.3 = (bf16[128,128]{1,0:T(8,128)(2,1)S(1)}, bf16[128,128]{1,0:T(8,128)(2,1)}, u32[]{:S(2)}) copy-start(bf16[128,128]{1,0:T(8,128)(2,1)} %keys_ref.1) | copy-start | bytes 98308
  1.5 0.8 copy-start.4
  2.3 5.4 %copy-start = (bf16[128,2048]{1,0:T(8,128)(2,1)S(1)}, bf16[128,2048]{1,0:T(8,128)(2,1)}, u32[]{:S(2)}) copy-start(bf16[128,2048]{1,0:T(8,128)(2,1)} %q_ref.1) | copy-start | bytes 1572868
  2.3 10.6 %collective-permute-start.2 = (bf16[128,256]{1,0:T(8,128)(2,1)S(1)}, bf16[128,256]{1,0:T(8,128)(2,1)S(1)}, u32[]{:S(2)}, u32[]{:S(2)}) collective-permute-start(bf16[128,256]{1,0:T(8,128)(2,1)S(1)} %shard_map.68), channel_id=1, source_target_pairs={{0,48},{16,0},{32,16},{48,32},{1,49},{17,1},{33,17},{49,33},{2,50}... | collective-permute-start | bytes 196616 | tf_op jit(solution)/shard_map/ppermute | solution.py:358
  7.0 6.3 %collective-permute-start.1 = (bf16[128,256]{1,0:T(8,128)(2,1)S(1)}, bf16[128,256]{1,0:T(8,128)(2,1)S(1)}, u32[]{:S(2)}, u32[]{:S(2)}) collective-permute-start(bf16[128,256]{1,0:T(8,128)(2,1)S(1)} %shard_map.68), channel_id=1, source_target_pairs={{0,32},{16,48},{32,0},{48,16},{1,33},{17,49},{33,1},{49,17},{2,34}... | collective-permute-start | bytes 196616 | tf_op jit(solution)/shard_map/ppermute | solution.py:358
  7.0 6.3 %collective-permute-start = (bf16[128,256]{1,0:T(8,128)(2,1)S(1)}, bf16[128,256]{1,0:T(8,128)(2,1)S(1)}, u32[]{:S(2)}, u32[]{:S(2)}) collective-permute-start(bf16[128,256]{1,0:T(8,128)(2,1)S(1)} %shard_map.68), channel_id=1, source_target_pairs={{0,16},{16,32},{32,48},{48,0},{1,17},{17,33},{33,49},{49,1},{2,18}... | collective-permute-start | bytes 196616 | tf_op jit(solution)/shard_map/ppermute | solution.py:358
  10.9 1.0 %copy-start.5 = (bf16[2048,256]{1,0:T(8,128)(2,1)}, bf16[2048,256]{1,0:T(8,128)(2,1)S(1)}, u32[]{:S(2)}) copy-start(bf16[2048,256]{1,0:T(8,128)(2,1)S(1)} %get-tuple-element.36.wk_ref) | copy-start | bytes 3145732
  11.9 1.0 %copy-start.7 = (bf16[2048,256]{1,0:T(8,128)(2,1)}, bf16[2048,256]{1,0:T(8,128)(2,1)S(1)}, u32[]{:S(2)}) copy-start(bf16[2048,256]{1,0:T(8,128)(2,1)S(1)} %get-tuple-element.31.wk_ref) | copy-start | bytes 3145732
  13.3 4.1 %collective-permute-start.6 = (bf16[512,256]{1,0:T(8,128)(2,1)S(1)}, bf16[512,256]{1,0:T(8,128)(2,1)S(1)}, u32[]{:S(2)}, u32[]{:S(2)}) collective-permute-start(bf16[512,256]{1,0:T(8,128)(2,1)S(1)} %pad_maximum_fusion.mine_ref), channel_id=1, source_target_pairs={{0,8},{8,0},{1,9},{9,1},{2,10},{10,2},{3,11},{11,3},{4,12},{12,4},... | collective-permute-start | bytes 786440 | tf_op jit(solution)/shard_map/ppermute | solution.py:358
  13.5 17.2 %copy-start.6 = (bf16[2048,256]{1,0:T(8,128)(2,1)S(1)}, bf16[2048,256]{1,0:T(8,128)(2,1)}, u32[]{:S(2)}) copy-start(bf16[2048,256]{1,0:T(8,128)(2,1)} %copy-done.5) | copy-start | bytes 3145732
  13.5 17.2 %collective-permute-start.5 = (bf16[512,256]{1,0:T(8,128)(2,1)S(1)}, bf16[512,256]{1,0:T(8,128)(2,1)S(1)}, u32[]{:S(2)}, u32[]{:S(2)}) collective-permute-start(bf16[512,256]{1,0:T(8,128)(2,1)S(1)} %pad_maximum_fusion.mine_ref), channel_id=1, source_target_pairs={{0,192},{64,0},{128,64},{192,128},{1,193},{65,1},{129,65},{193,129... | collective-permute-start | bytes 786440 | tf_op jit(solution)/shard_map/ppermute | solution.py:358
  14.3 16.4 %collective-permute-start.4 = (bf16[512,256]{1,0:T(8,128)(2,1)S(1)}, bf16[512,256]{1,0:T(8,128)(2,1)S(1)}, u32[]{:S(2)}, u32[]{:S(2)}) collective-permute-start(bf16[512,256]{1,0:T(8,128)(2,1)S(1)} %pad_maximum_fusion.mine_ref), channel_id=1, source_target_pairs={{0,128},{64,192},{128,0},{192,64},{1,129},{65,193},{129,1},{193,65... | collective-permute-start | bytes 786440 | tf_op jit(solution)/shard_map/ppermute | solution.py:358
  15.4 15.3 %collective-permute-start.3 = (bf16[512,256]{1,0:T(8,128)(2,1)S(1)}, bf16[512,256]{1,0:T(8,128)(2,1)S(1)}, u32[]{:S(2)}, u32[]{:S(2)}) collective-permute-start(bf16[512,256]{1,0:T(8,128)(2,1)S(1)} %pad_maximum_fusion.mine_ref), channel_id=1, source_target_pairs={{0,64},{64,128},{128,192},{192,0},{1,65},{65,129},{129,193},{193,1... | collective-permute-start | bytes 786440 | tf_op jit(solution)/shard_map/ppermute | solution.py:358
  17.4 1.2 %copy-start.8 = (bf16[2048,256]{1,0:T(8,128)(2,1)S(1)}, bf16[2048,256]{1,0:T(8,128)(2,1)}, u32[]{:S(2)}) copy-start(bf16[2048,256]{1,0:T(8,128)(2,1)} %copy-done.7) | copy-start | bytes 3145732
  43.0 15.7 %collective-permute-start.7 = (bf16[4096,256]{1,0:T(8,128)(2,1)S(1)}, bf16[4096,256]{1,0:T(8,128)(2,1)S(1)}, u32[]{:S(2)}, u32[]{:S(2)}) collective-permute-start(bf16[4096,256]{1,0:T(8,128)(2,1)S(1)} %shard_map.71.mine_ref), channel_id=1, source_target_pairs={{0,8},{8,0},{1,9},{9,1},{2,10},{10,2},{3,11},{11,3},{4,12},{12,4},... | collective-permute-start | bytes 6291464 | tf_op jit(solution)/shard_map/ppermute | solution.py:358
  43.1 4.5 %collective-permute-start.8 = (bf16[512,256]{1,0:T(8,128)(2,1)S(1)}, bf16[512,256]{1,0:T(8,128)(2,1)S(1)}, u32[]{:S(2)}, u32[]{:S(2)}) collective-permute-start(bf16[512,256]{1,0:T(8,128)(2,1)S(1)} %collective-permute-done.3.refs_0_), channel_id=1, source_target_pairs={{0,8},{8,0},{1,9},{9,1},{2,10},{10,2},{3,11},{11,3},{4,12},{12,4},... | collective-permute-start | bytes 786440 | tf_op jit(solution)/shard_map/ppermute | solution.py:358
  43.6 4.4 %collective-permute-start.9 = (bf16[512,256]{1,0:T(8,128)(2,1)S(1)}, bf16[512,256]{1,0:T(8,128)(2,1)S(1)}, u32[]{:S(2)}, u32[]{:S(2)}) collective-permute-start(bf16[512,256]{1,0:T(8,128)(2,1)S(1)} %collective-permute-done.4.refs_1_.refs_2_), channel_id=1, source_target_pairs={{0,8},{8,0},{1,9},{9,1},{2,10},{10,2},{3,11},{11,3},{4,12},{12,4},... | collective-permute-start | bytes 786440 | tf_op jit(solution)/shard_map/ppermute | solution.py:358
  43.7 4.7 %collective-permute-start.10 = (bf16[512,256]{1,0:T(8,128)(2,1)S(1)}, bf16[512,256]{1,0:T(8,128)(2,1)S(1)}, u32[]{:S(2)}, u32[]{:S(2)}) collective-permute-start(bf16[512,256]{1,0:T(8,128)(2,1)S(1)} %collective-permute-done.5.refs_2_.refs_4_), channel_id=1, source_target_pairs={{0,8},{8,0},{1,9},{9,1},{2,10},{10,2},{3,11},{11,3},{4,12},{12,4},... | collective-permute-start | bytes 786440 | tf_op jit(solution)/shard_map/ppermute | solution.py:358
where the time goes:
time: 79.9 us; the launch traced here: 79.6 us
  Pallas kernels  39.4 us (49%)
  blocking collectives  18.8 us (24%)
  starting transfers between devices  10.5 us (13%)
  local copies, waits for them, and re-layouts  4.8 us (6%)
  waiting for transfers between devices  4.73 us (6%)
    pallas_call x6, Pallas kernels, call(): pl.pallas_call(kernel, out_shape=outs, in_specs=ins or [SMEM] * scalars +...  39.4 us
    all_to_all x1, blocking collectives, body(): tiles = lax.all_to_all(loss[:, None, :], 'head', 0, 0, tiled=True)  18.8 us
    ppermute x11, starting transfers between devices, shifted(): return lax.ppermute(x, axis, [(i, (i + k) % n) for i in range(n)])  10.5 us
    unnamed x18, local copies, waits for them, and re-layouts  4.8 us
    ppermute x11, waiting for transfers between devices, shifted(): return lax.ppermute(x, axis, [(i, (i + k) % n) for i in range(n)])  4.73 us
  transfers between devices with their start and end apart: 11, of which 4 were waited for; matrix products, arithmetic and copies ran while one was open for 0% of the time, Pallas kernels for 32%

commit v1 on v0

v1 whole, which is shorter than its diff:
```python
import functools
import math

import jax
import jax.numpy as jnp
from jax import lax
from jax.experimental import pallas as pl
from jax.experimental.pallas import tpu as pltpu
from jax.sharding import Mesh
from jax.sharding import PartitionSpec as P


HQ = 128
D = 128
F = 2 * D
LOG2E = math.log2(math.e)
SCALE = LOG2E / math.sqrt(D)
NEG = -1e30
MOST = 67043328
SEQ = ("y", "z", "c")
F32, BF16 = jnp.float32, jnp.bfloat16
VMEM = pl.BlockSpec(memory_space=pltpu.VMEM)
SMEM = pl.BlockSpec(memory_space=pltpu.SMEM)
ANY = pl.BlockSpec(memory_space=pl.ANY)
HBM = pl.BlockSpec(memory_space=pltpu.HBM)


def mm(a, b):
    return jnp.dot(a, b, preferred_element_type=F32)


def mm_t(a, b):
    return lax.dot_general(a, b, (((1,), (1,)), ((), ())), preferred_element_type=F32)


def split(x):
    high = x.astype(BF16)
    return high, (x - high.astype(F32)).astype(BF16)


def both_softmax(x, axis):
    up = jnp.exp2(x - jnp.max(x, axis, keepdims=True))
    down = jnp.exp2(jnp.min(x, axis, keepdims=True) - x)
    up = up * (1.0 / jnp.sum(up, axis, keepdims=True))
    down = down * (1.0 / jnp.sum(down, axis, keepdims=True))
    return up.astype(BF16), down.astype(BF16)


def prepare(start, q_ref, fq_ref, q2_ref, qf_ref):
    tokens = q_ref.shape[0]

    def head(h, _):
        q = q_ref[:, pl.ds(pl.multiple_of(h * D, D), D)]
        rows = pl.ds(pl.multiple_of(h * tokens, tokens), tokens)
        high, low = split(q.astype(F32) * SCALE)
        q2_ref[rows, :D] = high
        q2_ref[rows, D:] = low
        up, down = both_softmax(mm(q, fq_ref[start + h]) * LOG2E, 1)
        qf_ref[rows, :D] = up
        qf_ref[rows, D:] = down
        return 0

    lax.fori_loop(0, q2_ref.shape[0] // tokens, head, 0, unroll=4)


def prepare_keys(fk_ref, wk_ref):
    def head(h, _):
        high, low = split((fk_ref[h].astype(F32) * LOG2E).T)
        rows = pl.ds(pl.multiple_of(h * D, D), D)
        wk_ref[rows, :D] = high
        wk_ref[rows, D:] = low
        return 0

    lax.fori_loop(0, fk_ref.shape[0], head, 0, unroll=4)


def lane_blocks(s):
    return [s[:, i : i + D] for i in range(0, s.shape[1], D)]


def row_max(parts):
    while len(parts) > 1:
        parts = [jnp.maximum(a, b) for a, b in zip(parts[::2], parts[1::2])]
    return jnp.max(parts[0], 1, keepdims=True)


def own_row(start, at_ref, q2_ref, qf_ref, wk_ref, *refs):
    rows, refs = refs[:-17], refs[-17:]
    acc_ref, m_ref, near_ref, k2, v1, bias, keep = refs[:7]
    s0, s1, x0, x1, f0, f1, p0, p1, a0, a1 = refs[7:]
    tokens = keep.shape[0]
    heads = qf_ref.shape[0] // tokens
    half = rows[0].shape[0]
    wide = k2.shape[0]
    many = s0.shape[0] // tokens
    groups = heads // many
    tile = wide // many
    z, c = at_ref[1], at_ref[2]
    safe = jnp.broadcast_to(rows[0][:16, :D].astype(F32)[:1], (tokens, D))
    for side, ref in enumerate(rows):
        for slot in range(half // tokens):
            kv = ref[slot * tokens : (slot + 1) * tokens].astype(F32)
            key, value, one = kv[:, :D], kv[:, D:], jnp.ones((tokens, D), F32)
            if slot or side:
                seen = slot <= z if slot else c == 1
                key = jnp.where(seen, key, safe)
                value = jnp.where(seen, value, 0.0)
                one = jnp.where(seen, one, 0.0)
            here = slice(side * half + slot * tokens, side * half + (slot + 1) * tokens)
            k2[here, :D] = key.astype(BF16)
            k2[here, D:] = key.astype(BF16)
            v1[here, :D] = value.astype(BF16)
            v1[here, D:] = one.astype(BF16)
    row = lax.broadcasted_iota(jnp.int32, (tokens, tokens), 0)
    col = lax.broadcasted_iota(jnp.int32, (tokens, tokens), 1)
    seen = (col <= row).astype(F32)
    keep[...] = seen
    bias[...] = (1.0 - seen) * NEG

    def block(g, size):
        return pl.ds(pl.multiple_of(g * size, size), size)

    def first(g, s, x, j):
        cols = slice(j * tile, (j + 1) * tile)
        s[:, cols] = mm_t(q2_ref[block(g, many * tokens)], k2[cols])
        x[:, cols] = mm_t(wk_ref[block(start // many + g, many * D)], k2[cols])

    def second(g, s, x, p, f, i):
        here = slice(i * tokens, (i + 1) * tokens)
        parts = lane_blocks(s[here])
        parts[0] = parts[0] + bias[...]
        m = row_max(parts)
        m_ref[block(g * many + i, tokens)] = jnp.broadcast_to(m, (tokens, D))
        p[here] = jnp.concatenate([jnp.exp2(a - m).astype(BF16) for a in parts], 1)
        up, down = both_softmax(x[i * D : (i + 1) * D], 0)
        f[i * F : i * F + D] = up
        f[i * F + D : (i + 1) * F] = down

    def third(g, f, a, i):
        here = slice(i * tokens, (i + 1) * tokens)
        scores = mm(qf_ref[block(g * many + i, tokens)], f[i * F : (i + 1) * F])
        a[here, :D] = (scores[:, :D] * keep[...]).astype(BF16)
        a[here, D:] = scores[:, D:].astype(BF16)

    def mix(out_ref, g, p):
        out_ref[block(g, many * tokens)] = mm(p[...], v1[...])

    def stage(g, s, x, p, f, s_next, x_next, p_last, f_last, a_last, a_older):
        last, older = jnp.maximum(g - 1, 0), jnp.maximum(g - 2, 0)
        for j in range(many):
            first(jnp.minimum(g + 1, groups - 1), s_next, x_next, j)
            second(g, s, x, p, f, j)
            third(last, f_last, a_last, j)
            if j == 0:
                mix(acc_ref, last, p_last)
            if j == many // 2:
                mix(near_ref, older, a_older)

    for j in range(many):
        first(0, s0, x0, j)
    f1[...] = jnp.zeros_like(f1)
    p1[...] = jnp.zeros_like(p1)
    a0[...] = jnp.zeros_like(a0)

    def step(i, _):
        g = 2 * i
        stage(g, s0, x0, p0, f0, s1, x1, p1, f1, a1, a0)
        stage(g + 1, s1, x1, p1, f1, s0, x0, p0, f0, a0, a1)
        return 0

    lax.fori_loop(0, groups // 2, step, 0)
    mix(acc_ref, groups - 1, p1)
    mix(near_ref, groups - 2, a0)
    for j in range(many):
        third(groups - 1, f1, a1, j)
    mix(near_ref, groups - 1, a1)


def absolute(at_ref, rows, store):
    depth = len(rows)
    y = at_ref[0]
    places = (y, depth - 1 - y, y + 1 - 2 * lax.rem(y, 2), lax.rem(y + depth // 2, depth))
    for r, refs in zip(places, rows):

        @pl.when(r < depth - 1)
        def _(r=r, refs=refs):
            store(r, refs)


def fill_at(k2, v1, at, size, kv):
    here = pl.ds(pl.multiple_of(at, size), size)
    k2[here, :D] = kv[:, :D]
    k2[here, D:] = kv[:, :D]
    v1[here, :D] = kv[:, D:]
    v1[here, D:] = jnp.ones((size, D), BF16)


def unit_of(at_ref, u, half_heads):
    mine = u < at_ref[0]
    return jnp.where(mine, u, u - at_ref[0]), jnp.where(mine, 0, half_heads)


def earlier_state(at_ref, wk_ref, *refs):
    rows, (out_ref, k2, v1, state, x0, x1, f0, f1) = refs[:-8], refs[-8:]
    heads = out_ref.shape[0] // F
    half = rows[0].shape[0]
    pairs = heads // 4
    count = (len(rows) - 1) * pairs
    state[...] = jnp.zeros_like(state)
    f1[...] = jnp.zeros_like(f1)
    absolute(at_ref, rows, lambda r, ref: fill_at(k2, v1, r * half, half, ref[...]))

    def place(t):
        t = jnp.clip(t, 0, count - 1)
        r, head = unit_of(at_ref, lax.div(t, pairs), heads // 2)
        head = head + 2 * lax.rem(t, pairs)
        return pl.ds(pl.multiple_of(r * half, half), half), head

    def first(t, x):
        at, head = place(t)
        x[...] = mm_t(wk_ref[pl.ds(pl.multiple_of(head * D, 2 * D), 2 * D)], k2[at])

    def second(x, f):
        for i in range(2):
            up, down = both_softmax(x[i * D : (i + 1) * D], 0)
            f[i * F : i * F + D] = up
            f[i * F + D : (i + 1) * F] = down

    def third(t, f):
        at, head = place(t)
        state[pl.ds(pl.multiple_of(head * F, 2 * F), 2 * F)] += mm(f[...], v1[at])

    first(0, x0)

    def step(i, _):
        t = 2 * i
        first(t + 1, x1)
        second(x0, f0)
        third(t - 1, f1)
        first(t + 2, x0)
        second(x1, f1)
        third(t, f0)
        return 0

    lax.fori_loop(0, count // 2, step, 0)
    third(count - 1, f1)
    out_ref[...] = state[...].astype(BF16)


def earlier_teacher(at_ref, q2a_ref, q2b_ref, acca_ref, accb_ref, ma_ref, mb_ref, *refs):
    rows, (acc, k2, v1, q2, m_all, s0, s1, p0, p1) = refs[:-9], refs[-9:]
    half = rows[0].shape[0]
    wide = 2 * half
    part = s0.shape[0]
    side = q2a_ref.shape[0]
    groups = side // part
    pairs = [rows[i : i + 2] for i in range(0, len(rows), 2)]
    count = (len(pairs) - 1) * groups
    for i, (q2_ref, acc_ref, m_ref) in enumerate(
        ((q2a_ref, acca_ref, ma_ref), (q2b_ref, accb_ref, mb_ref))
    ):
        here = slice(i * side, (i + 1) * side)
        q2[here] = q2_ref[...]
        acc[here] = acc_ref[...]
        m_all[here] = m_ref[...]

    def store(r, pair):
        for i, ref in enumerate(pair):
            fill_at(k2, v1, r * wide + i * half, half, ref[...])

    absolute(at_ref, pairs, store)

    def place(t):
        t = jnp.clip(t, 0, count - 1)
        r, at = unit_of(at_ref, lax.div(t, groups), side)
        at = pl.multiple_of(at + lax.rem(t, groups) * part, part)
        return pl.ds(pl.multiple_of(r * wide, wide), wide), at

    def first(t, s):
        at, g = place(t)
        s[...] = mm_t(q2[pl.ds(g, part)], k2[at])

    def second(t, s, p):
        _, g = place(t)
        for i in range(0, part, D):
            here = pl.ds(pl.multiple_of(g + i, D), D)
            before = m_all[here]
            m = jnp.maximum(before, row_max(lane_blocks(s[i : i + D])))
            m_all[here] = m
            factor = jnp.exp2(before - m)
            acc[here] = acc[here] * jnp.concatenate([factor, factor], 1)
            m = jnp.concatenate([m] * (wide // D), 1)
            p[i : i + D] = jnp.exp2(s[i : i + D] - m).astype(BF16)

    def third(t, p):
        at, g = place(t)
        acc[pl.ds(g, part)] += mm(p[...], v1[at])

    first(0, s0)

    def step(i, _):
        t = 2 * i
        first(t + 1, s1)
        second(t, s0, p0)
        third(t, p0)
        first(t + 2, s0)
        second(t + 1, s1, p1)
        third(t + 1, p1)
        return 0

    lax.fori_loop(0, count // 2, step, 0)


def by_place(total, blocks, width):
    tokens = total.shape[0]
    per_token = jnp.sum(total.T, 0, keepdims=True) * (1.0 / HQ)
    t = lax.broadcasted_iota(jnp.int32, (blocks, tokens), 1)
    b = lax.broadcasted_iota(jnp.int32, (blocks, tokens), 0)
    own = (t >= b * width) & (t < (b + 1) * width)
    ti = lax.broadcasted_iota(jnp.int32, (tokens, width), 0)
    ji = lax.broadcasted_iota(jnp.int32, (tokens, width), 1)
    pick = jnp.zeros((tokens, width), F32)
    for i in range(blocks):
        pick = pick + (ti == ji + i * width).astype(F32)
    return jnp.dot(
        jnp.where(own, jnp.broadcast_to(per_token, (blocks, tokens)), 0.0),
        pick,
        precision=lax.Precision.HIGHEST,
        preferred_element_type=F32,
    )


def finish(start, qf_ref, near_ref, mine_ref, other_ref, acc_ref, out_ref, loss_ref, total):
    tokens = total.shape[0]
    total[...] = jnp.zeros_like(total)
    for h in range(qf_ref.shape[0] // tokens):
        here = slice(h * tokens, (h + 1) * tokens)
        there = slice((start + h) * F, (start + h + 1) * F)
        qf = qf_ref[here]
        sums = near_ref[here] + mm(qf, mine_ref[there]) + mm(qf, other_ref[there])
        student = sums[:, :D] * (1.0 / sums[:, D:])
        out_ref[:, h * D : (h + 1) * D] = student.astype(BF16)
        acc = acc_ref[(start + h) * tokens : (start + h + 1) * tokens]
        total[...] += (student - acc[:, :D] * (1.0 / acc[:, D:])) ** 2
    loss_ref[...] = by_place(total[...], *loss_ref.shape)


def finish_mine(qf_ref, near_ref, mine_ref, other_ref, acc_ref, student_ref, loss_ref, total, out, sem):
    finish(0, qf_ref, near_ref, mine_ref, other_ref, acc_ref, out, loss_ref, total)
    copy = pltpu.make_async_copy(out, student_ref.at[:, : out.shape[1]], sem)
    copy.start()
    copy.wait()


def move(pairs, sems):
    copies = [pltpu.make_async_copy(a, b, sems.at[i]) for i, (a, b) in enumerate(pairs)]
    for copy in copies:
        copy.start()
    for copy in copies:
        copy.wait()


def stack(*refs):
    size = refs[0].shape[0]
    for i, ref in enumerate(refs[:-1]):
        refs[-1][i * size : (i + 1) * size] = ref[...]


def pack(at_ref, keys_ref, values_ref, kv_ref, sems):
    move(((keys_ref, kv_ref.at[:, :D]), (values_ref, kv_ref.at[:, D:])), sems)


def halve(q_ref, part_ref):
    part_ref[...] = q_ref[:, part_ref.shape[1] :]


def join(back_ref, student_ref, out_ref, sem):
    copy = pltpu.make_async_copy(back_ref, out_ref.at[:, back_ref.shape[1] :], sem)
    copy.start()
    copy.wait()


def call(kernel, outs, scratch, us, mib, *args, scalars=0, ins=None, spec=None, aliases=None):
    return pl.pallas_call(
        kernel,
        out_shape=outs,
        in_specs=ins or [SMEM] * scalars + [VMEM] * (len(args) - scalars),
        out_specs=spec or jax.tree.map(lambda _: VMEM, outs),
        scratch_shapes=scratch,
        input_output_aliases=aliases or {},
        cost_estimate=pl.CostEstimate(
            flops=int(us * 1e9), bytes_accessed=1 << 20, transcendentals=0
        ),
        compiler_params=pltpu.CompilerParams(vmem_limit_bytes=min(mib << 20, MOST)),
    )(*args)


def shape(dims, dtype=F32):
    return jax.ShapeDtypeStruct(dims, dtype)


def shifted(x, axis, k):
    n = lax.axis_size(axis)
    return lax.ppermute(x, axis, [(i, (i + k) % n) for i in range(n)])


def mirrored(x, axis):
    n = lax.axis_size(axis)
    return lax.ppermute(x, axis, [(i, n - 1 - i) for i in range(n)])


def body(queries, keys, values, feat_q, feat_k):
    tokens = queries.shape[0]
    heads = feat_q.shape[0]
    side = heads // 2
    depth = lax.axis_size("y")
    at = jnp.stack([lax.axis_index(a) for a in SEQ]).astype(jnp.int32)
    rows = side * tokens
    kv = call(
        pack,
        shape((tokens, F), BF16),
        [pltpu.SemaphoreType.DMA((2,))],
        1,
        1,
        at,
        pltpu.with_memory_space_constraint(keys, pltpu.HBM),
        pltpu.with_memory_space_constraint(values, pltpu.HBM),
        ins=[SMEM] + [HBM] * 2,
    )
    zs = [shifted(kv, "z", k) for k in range(1, lax.axis_size("z"))]
    part = call(halve, shape((tokens, side * D), BF16), [], 0.2, 2, queries)
    part = mirrored(part, "y")
    wk = call(prepare_keys, shape((heads * D, F), BF16), [], 1, 4, feat_k)
    halves = (shape((rows, F), BF16),) * 2
    q2a, qfa = call(functools.partial(prepare, 0), halves, [], 1.5, 4, queries, feat_q)
    zs, wk, q2a, qfa = lax.optimization_barrier((zs, wk, q2a, qfa))
    half = tokens * (1 + len(zs))
    row = call(stack, shape((half, F), BF16), [], 0.1, 2, kv, *zs)
    other = shifted(row, "c", 1)
    partner = mirrored(row, "y")
    next_row = lax.ppermute(row, "y", [(i, i ^ 1) for i in range(depth)])
    far_row = shifted(row, "y", depth // 2)
    many = 2

    def near_part(start, q2, qf, *sources):
        return call(
            functools.partial(own_row, start),
            (shape((rows, F)), shape((rows, D)), shape((rows, F))),
            [pltpu.VMEM((2 * half, F), BF16)] * 2
            + [pltpu.VMEM((tokens, tokens), F32)] * 2
            + [pltpu.VMEM((many * tokens, 2 * half), F32)] * 4
            + [pltpu.VMEM((many * F, 2 * half), BF16)] * 2
            + [pltpu.VMEM((many * tokens, 2 * half), BF16)] * 4,
            6,
            18,
            at,
            q2,
            qf,
            wk,
            *sources,
            scalars=1,
        )

    acca, ma, neara = near_part(0, q2a, qfa, row, other)
    part, partner, acca = lax.optimization_barrier((part, partner, acca))
    partner_other = shifted(partner, "c", 1)
    q2b, qfb = call(functools.partial(prepare, side), halves, [], 1.5, 4, part, feat_q)
    accb, mb, nearb = near_part(side, q2b, qfb, partner, partner_other)
    above = (next_row, far_row)
    above, acca, accb = lax.optimization_barrier((above, acca, accb))
    above_other = []
    for a in above:
        above_other.append(shifted(a, "c", 1))
    above = [partner, *above]
    above_other = [partner_other, *above_other]
    earlier = (depth - 1) * half
    state = call(
        earlier_state,
        shape((heads * F, F), BF16),
        [pltpu.VMEM((earlier, F), BF16)] * 2
        + [pltpu.VMEM((heads * F, F), F32)]
        + [pltpu.VMEM((2 * D, half), F32)] * 2
        + [pltpu.VMEM((2 * F, half), BF16)] * 2,
        6,
        14,
        at,
        wk,
        row,
        *above,
        scalars=1,
    )
    state_other = shifted(state, "c", 1)
    pairs = [r for pair in zip([row, *above], [other, *above_other]) for r in pair]
    acc = call(
        earlier_teacher,
        shape((2 * rows, F)),
        [pltpu.VMEM((2 * earlier, F), BF16)] * 2
        + [pltpu.VMEM((2 * rows, F), BF16), pltpu.VMEM((2 * rows, D), F32)]
        + [pltpu.VMEM((4 * tokens, 2 * half), F32)] * 2
        + [pltpu.VMEM((4 * tokens, 2 * half), BF16)] * 2,
        6,
        18,
        at,
        q2a,
        q2b,
        acca,
        accb,
        ma,
        mb,
        *pairs,
        scalars=1,
    )
    parts = lax.axis_size("x") * lax.axis_size("w")
    grid = (parts, tokens // parts)
    part_shape = shape((tokens, side * D), BF16)
    theirs, loss_b = call(
        functools.partial(finish, side),
        (part_shape, shape(grid)),
        [pltpu.VMEM((tokens, D), F32)],
        1,
        4,
        qfb,
        nearb,
        state,
        state_other,
        acc,
    )
    loss_b = mirrored(loss_b, "y")
    back = mirrored(theirs, "y")
    student, loss = call(
        finish_mine,
        (shape((tokens, heads * D), BF16), shape(grid)),
        [
            pltpu.VMEM((tokens, D), F32),
            pltpu.VMEM((tokens, side * D), BF16),
            pltpu.SemaphoreType.DMA,
        ],
        1,
        4,
        qfa,
        neara,
        state,
        state_other,
        acc,
        spec=(ANY, VMEM),
    )
    loss = loss + loss_b
    tiles = lax.all_to_all(loss[:, None, :], ("x", "w"), 0, 0, tiled=True)
    token_loss = jnp.sum(tiles, axis=(0, 1))
    student = call(
        join,
        shape((tokens, heads * D), BF16),
        [pltpu.SemaphoreType.DMA],
        1,
        2,
        back,
        student,
        ins=[VMEM, ANY],
        spec=ANY,
        aliases={1: 0},
    )
    return student, token_loss


def solution(mesh):
    grid = Mesh(mesh.devices.reshape(4, 4, 2, 4, 2), (*SEQ, "x", "w"))
    head = ("x", "w")
    placed = P(SEQ, head)
    return jax.shard_map(
        body,
        mesh=grid,
        in_specs=(placed, placed, placed, P(head), P(head)),
        out_specs=(placed, P((*SEQ, *head))),
        check_vma=False,
    )
```

time: 79.9 us -> 93.3 us (1.17)
  the two profiles are of different devices: /device:TPU:24 before, /device:TPU:2 now
where the time goes in v1:
time: 93.3 us; the launch traced here: 93.2 us
  Pallas kernels  33.6 us (36%)
  waiting for transfers between devices  23.4 us (25%)
  blocking collectives  17.9 us (19%)
  starting transfers between devices  16.6 us (18%)
  between operations  0.97 us (1%)
    pallas_call x13, Pallas kernels, call(): pl.pallas_call(kernel, out_shape=outs, in_specs=ins or [SMEM] * scalars +...  33.6 us
    all_to_all x1, blocking collectives, body(): tiles = lax.all_to_all(loss[:, None, :], ('x', 'w'), 0, 0, tiled=True)  17.9 us
    ppermute x4, waiting for transfers between devices, mirrored(): return lax.ppermute(x, axis, [(i, n - 1 - i) for i in range(n)])  10.7 us
    ppermute x9, waiting for transfers between devices, shifted(): return lax.ppermute(x, axis, [(i, (i + k) % n) for i in range(n)])  8.33 us
    ppermute x9, starting transfers between devices, shifted(): return lax.ppermute(x, axis, [(i, (i + k) % n) for i in range(n)])  8.08 us
    ppermute x4, starting transfers between devices, mirrored(): return lax.ppermute(x, axis, [(i, n - 1 - i) for i in range(n)])  6.62 us
    ppermute x1, waiting for transfers between devices, body(): next_row = lax.ppermute(row, 'y', [(i, i ^ 1) for i in range(depth)])  4.4 us
    ppermute x1, starting transfers between devices, body(): next_row = lax.ppermute(row, 'y', [(i, i ^ 1) for i in range(depth)])  1.89 us
  transfers between devices with their start and end apart: 14, of which 8 were waited for; matrix products, arithmetic and copies ran while one was open for 1% of the time, Pallas kernels for 25%

profile of v1, /device:TPU:2, one launch (start us, length us, event | category | flops | bytes accessed | tf_op | source)
XLA Modules:
  0.0 93.2 jit_solution(18371436352423938821)
XLA Ops:
  0.7 1.3 %shard_map.69.refs_0_ = bf16[128,256]{1,0:T(8,128)(2,1)S(1)} custom-call(s32[3]{0:T(128)S(1)} %pad_add_fusion.at_ref, bf16[128,128]{1,0:T(8,128)(2,1)} %keys_ref.1, bf16[128,128]{1,0:T(8,128)(2,1)} %values_ref.1), custom_call_target="tpu_custom_call" | custom-call | flops 1000000000 | bytes 1048576 | tf_op jit(solution)/shard_map/pallas_call | solution.py:384
  2.1 4.7 %collective-permute-start.3 = (bf16[128,256]{1,0:T(8,128)(2,1)S(1)}, bf16[128,256]{1,0:T(8,128)(2,1)S(1)}, u32[]{:S(2)}, u32[]{:S(2)}) collective-permute-start(bf16[128,256]{1,0:T(8,128)(2,1)S(1)} %shard_map.69.refs_0_), channel_id=1, source_target_pairs={{0,48},{16,0},{32,16},{48,32},{1,49},{17,1},{33,17},{49,33},{2,50}... | collective-permute-start | bytes 196616 | tf_op jit(solution)/shard_map/ppermute | solution.py:404
  6.8 0.7 collective-permute-start.1
  7.5 1.0 %shard_map.71 = (bf16[1024,256]{1,0:T(8,128)(2,1)S(1)}, bf16[1024,256]{1,0:T(8,128)(2,1)S(1)}) custom-call(bf16[128,2048]{1,0:T(8,128)(2,1)S(1)} %copy-done, bf16[16,128,128]{2,1,0:T(8,128)(2,1)S(1)} %copy-done.2), custom_call_target="tpu_custom_call" | custom-call | flops 1500000000 | bytes 1048576 | tf_op jit(solution)/shard_map/pallas_call | solution.py:384
  8.5 0.6 shard_map.70.wk_ref
  9.3 3.8 %collective-permute-done.2.refs_2_ = bf16[128,256]{1,0:T(8,128)(2,1)S(1)} collective-permute-done((bf16[128,256]{1,0:T(8,128)(2,1)S(1)}, bf16[128,256]{1,0:T(8,128)(2,1)S(1)}, u32[]{:S(2)}, u32[]{:S(2)}) %collective-permute-start.2) | collective-permute-done | bytes 65568 | tf_op jit(solution)/shard_map/ppermute | solution.py:404
  13.2 3.1 %collective-permute-start = (bf16[128,1024]{1,0:T(8,128)(2,1)S(1)}, bf16[128,1024]{1,0:T(8,128)(2,1)S(1)}, u32[]{:S(2)}, u32[]{:S(2)}) collective-permute-start(bf16[128,1024]{1,0:T(8,128)(2,1)S(1)} %shard_map.68), channel_id=1, source_target_pairs={{0,192},{64,128},{128,64},{192,0},{1,193},{65,129},{129,65},{193,1... | collective-permute-start | bytes 786440 | tf_op jit(solution)/shard_map/ppermute | solution.py:409
  16.6 6.8 %shard_map.73 = (f32[1024,256]{1,0:T(8,128)S(1)}, f32[1024,128]{1,0:T(8,128)S(1)}, f32[1024,256]{1,0:T(8,128)S(1)}) custom-call(s32[3]{0:T(128)S(1)} %pad_add_fusion.at_ref, bf16[1024,256]{1,0:T(8,128)(2,1)S(1)} %get-tuple-element.34.q2_ref.q2a_ref, bf16[1024,256]{1,0:T(8,128)(2,1)S(1)} %get-tuple-element.35.qf_ref, bf16[2048,256]{1,0:T(8,128)(2,1)S(1)} %shard_map.70.wk_ref, ...), custom_call_target="tpu_custom_call" | custom-call | flops 6000000000 | bytes 1048576 | tf_op jit(solution)/shard_map/pallas_call | solution.py:384
  23.7 5.2 %collective-permute-done.4.refs_0_.refs_1_.refs_2_ = bf16[512,256]{1,0:T(8,128)(2,1)S(1)} collective-permute-done((bf16[512,256]{1,0:T(8,128)(2,1)S(1)}, bf16[512,256]{1,0:T(8,128)(2,1)S(1)}, u32[]{:S(2)}, u32[]{:S(2)}) %collective-permute-start.4) | collective-permute-done | bytes 262176 | tf_op jit(solution)/shard_map/ppermute | solution.py:409
  28.9 1.9 %collective-permute-start.8 = (bf16[512,256]{1,0:T(8,128)(2,1)S(1)}, bf16[512,256]{1,0:T(8,128)(2,1)S(1)}, u32[]{:S(2)}, u32[]{:S(2)}) collective-permute-start(bf16[512,256]{1,0:T(8,128)(2,1)S(1)} %shard_map.72.refs_0_), channel_id=1, source_target_pairs={{0,128},{64,192},{128,0},{192,64},{1,129},{65,193},{129,1},{193,65... | collective-permute-start | bytes 786440 | tf_op jit(solution)/shard_map/ppermute | solution.py:404
  30.9 1.9 %collective-permute-start.7 = (bf16[512,256]{1,0:T(8,128)(2,1)S(1)}, bf16[512,256]{1,0:T(8,128)(2,1)S(1)}, u32[]{:S(2)}, u32[]{:S(2)}) collective-permute-start(bf16[512,256]{1,0:T(8,128)(2,1)S(1)} %shard_map.72.refs_0_), channel_id=1, source_target_pairs={{0,64},{64,0},{128,192},{192,128},{1,65},{65,1},{129,193},{193,129... | collective-permute-start | bytes 786440 | tf_op jit(solution)/shard_map/ppermute | solution.py:441
  32.7 1.0 %shard_map.74 = (bf16[1024,256]{1,0:T(8,128)(2,1)S(1)}, bf16[1024,256]{1,0:T(8,128)(2,1)S(1)}) custom-call(bf16[128,1024]{1,0:T(8,128)(2,1)S(1)} %collective-permute-done.q_ref, bf16[16,128,128]{2,1,0:T(8,128)(2,1)S(1)} %copy-done.2), custom_call_target="tpu_custom_call" | custom-call | flops 1500000000 | bytes 1048576 | tf_op jit(solution)/shard_map/pallas_call | solution.py:384
  33.7 6.9 %shard_map.75 = (f32[1024,256]{1,0:T(8,128)S(1)}, f32[1024,128]{1,0:T(8,128)S(1)}, f32[1024,256]{1,0:T(8,128)S(1)}) custom-call(s32[3]{0:T(128)S(1)} %pad_add_fusion.at_ref, bf16[1024,256]{1,0:T(8,128)(2,1)S(1)} %get-tuple-element.40.q2_ref.q2b_ref, bf16[1024,256]{1,0:T(8,128)(2,1)S(1)} %get-tuple-element.39.qf_ref, bf16[2048,256]{1,0:T(8,128)(2,1)S(1)} %shard_map.70.wk_ref, ...), custom_call_target="tpu_custom_call" | custom-call | flops 6000000000 | bytes 1048576 | tf_op jit(solution)/shard_map/pallas_call | solution.py:384
  40.7 4.4 %collective-permute-done.7.refs_2_.refs_4_ = bf16[512,256]{1,0:T(8,128)(2,1)S(1)} collective-permute-done((bf16[512,256]{1,0:T(8,128)(2,1)S(1)}, bf16[512,256]{1,0:T(8,128)(2,1)S(1)}, u32[]{:S(2)}, u32[]{:S(2)}) %collective-permute-start.7) | collective-permute-done | bytes 262176 | tf_op jit(solution)/shard_map/ppermute | solution.py:441
  45.0 7.2 %shard_map.76.mine_ref = bf16[4096,256]{1,0:T(8,128)(2,1)S(1)} custom-call(s32[3]{0:T(128)S(1)} %pad_add_fusion.at_ref, bf16[2048,256]{1,0:T(8,128)(2,1)S(1)} %shard_map.70.wk_ref, bf16[512,256]{1,0:T(8,128)(2,1)S(1)} %shard_map.72.refs_0_, bf16[512,256]{1,0:T(8,128)(2,1)S(1)} %collective-permute-done.4.refs_0_.refs_1_.refs_2_, ...), custom_call_target="tpu_custom_call" | custom-call | flops 6000000000 | bytes 1048576 | tf_op jit(solution)/shard_map/pallas_call | solution.py:384
  53.0 3.9 %collective-permute-done.10.refs_5_ = bf16[512,256]{1,0:T(8,128)(2,1)S(1)} collective-permute-done((bf16[512,256]{1,0:T(8,128)(2,1)S(1)}, bf16[512,256]{1,0:T(8,128)(2,1)S(1)}, u32[]{:S(2)}, u32[]{:S(2)}) %collective-permute-start.10) | collective-permute-done | bytes 262176 | tf_op jit(solution)/shard_map/ppermute | solution.py:404
  57.3 6.1 %shard_map.77.acc_ref = f32[2048,256]{1,0:T(8,128)S(1)} custom-call(s32[3]{0:T(128)S(1)} %pad_add_fusion.at_ref, bf16[1024,256]{1,0:T(8,128)(2,1)S(1)} %get-tuple-element.34.q2_ref.q2a_ref, bf16[1024,256]{1,0:T(8,128)(2,1)S(1)} %get-tuple-element.40.q2_ref.q2b_ref, f32[1024,256]{1,0:T(8,128)S(1)} %get-tuple-element.47.acca_ref, ...), custom_call_target="tpu_custom_call" | custom-call | flops 6000000000 | bytes 1048576 | tf_op jit(solution)/shard_map/pallas_call | solution.py:384
  63.4 0.7 shard_map.78
  64.5 2.9 %collective-permute-start.13 = (f32[8,16]{1,0:T(8,128)S(1)}, f32[8,16]{1,0:T(8,128)S(1)}, u32[]{:S(2)}, u32[]{:S(2)}) collective-permute-start(f32[8,16]{1,0:T(8,128)S(1)} %get-tuple-element.55), channel_id=1, source_target_pairs={{0,192},{64,128},{128,64},{192,0},{1,193},{65,129},{129,65},{193,1... | collective-permute-start | bytes 1544 | tf_op jit(solution)/shard_map/ppermute | solution.py:409
  67.4 1.2 %shard_map.79 = (bf16[128,2048]{1,0:T(8,128)(2,1)}, f32[8,16]{1,0:T(8,128)S(1)}) custom-call(bf16[1024,256]{1,0:T(8,128)(2,1)S(1)} %get-tuple-element.35.qf_ref, f32[1024,256]{1,0:T(8,128)S(1)} %get-tuple-element.52.near_ref, bf16[4096,256]{1,0:T(8,128)(2,1)S(1)} %shard_map.76.mine_ref, bf16[4096,256]{1,0:T(8,128)(2,1)S(1)} %collective-permute-done.9.other_ref, ...), custom_call_target="tpu_custom_call" | custom-call | flops 1000000000 | bytes 1048576 | tf_op jit(solution)/shard_map/pallas_call | solution.py:384
  68.6 5.2 %collective-permute-done.13 = f32[8,16]{1,0:T(8,128)S(1)} collective-permute-done((f32[8,16]{1,0:T(8,128)S(1)}, f32[8,16]{1,0:T(8,128)S(1)}, u32[]{:S(2)}, u32[]{:S(2)}) %collective-permute-start.13) | collective-permute-done | bytes 544 | tf_op jit(solution)/shard_map/ppermute | solution.py:409
  73.8 17.9 %all_to_all.5 = f32[8,1,16]{2,1,0:T(1,128)S(1)} all-to-all(f32[8,1,16]{2,1,0:T(1,128)S(1)} %bitcast.6), channel_id=1, replica_groups=mesh['y'=4,'z'=4,'c'=2,'x'=4,'w'=2] {'x','w'}, dimensions={0} | all-to-all | bytes 1024 | tf_op jit(solution)/shard_map/all_to_all | solution.py:548
  91.7 0.5 reduce_sum.9
  92.3 0.7 shard_map.80
  (27 shorter events, 2.4 us)
Async XLA Ops:
  0.6 6.8 %copy-start.2 = (bf16[16,128,128]{2,1,0:T(8,128)(2,1)S(1)}, bf16[16,128,128]{2,1,0:T(8,128)(2,1)}, u32[]{:S(2)}) copy-start(bf16[16,128,128]{2,1,0:T(8,128)(2,1)} %fq_ref.3) | copy-start | bytes 1572868
  0.6 6.8 %copy-start = (bf16[128,2048]{1,0:T(8,128)(2,1)S(1)}, bf16[128,2048]{1,0:T(8,128)(2,1)}, u32[]{:S(2)}) copy-start(bf16[128,2048]{1,0:T(8,128)(2,1)} %q_ref.3) | copy-start | bytes 1572868
  2.1 6.4 %copy-start.1 = (bf16[16,128,128]{2,1,0:T(8,128)(2,1)S(1)}, bf16[16,128,128]{2,1,0:T(8,128)(2,1)}, u32[]{:S(2)}) copy-start(bf16[16,128,128]{2,1,0:T(8,128)(2,1)} %fk_ref.1) | copy-start | bytes 1572868
  2.1 7.2 %collective-permute-start.3 = (bf16[128,256]{1,0:T(8,128)(2,1)S(1)}, bf16[128,256]{1,0:T(8,128)(2,1)S(1)}, u32[]{:S(2)}, u32[]{:S(2)}) collective-permute-start(bf16[128,256]{1,0:T(8,128)(2,1)S(1)} %shard_map.69.refs_0_), channel_id=1, source_target_pairs={{0,48},{16,0},{32,16},{48,32},{1,49},{17,1},{33,17},{49,33},{2,50}... | collective-permute-start | bytes 196616 | tf_op jit(solution)/shard_map/ppermute | solution.py:404
  6.8 6.3 %collective-permute-start.2 = (bf16[128,256]{1,0:T(8,128)(2,1)S(1)}, bf16[128,256]{1,0:T(8,128)(2,1)S(1)}, u32[]{:S(2)}, u32[]{:S(2)}) collective-permute-start(bf16[128,256]{1,0:T(8,128)(2,1)S(1)} %shard_map.69.refs_0_), channel_id=1, source_target_pairs={{0,32},{16,48},{32,0},{48,16},{1,33},{17,49},{33,1},{49,17},{2,34}... | collective-permute-start | bytes 196616 | tf_op jit(solution)/shard_map/ppermute | solution.py:404
  6.8 6.3 %collective-permute-start.1 = (bf16[128,256]{1,0:T(8,128)(2,1)S(1)}, bf16[128,256]{1,0:T(8,128)(2,1)S(1)}, u32[]{:S(2)}, u32[]{:S(2)}) collective-permute-start(bf16[128,256]{1,0:T(8,128)(2,1)S(1)} %shard_map.69.refs_0_), channel_id=1, source_target_pairs={{0,16},{16,32},{32,48},{48,0},{1,17},{17,33},{33,49},{49,1},{2,18}... | collective-permute-start | bytes 196616 | tf_op jit(solution)/shard_map/ppermute | solution.py:404
  13.1 3.5 %collective-permute-start.5 = (bf16[512,256]{1,0:T(8,128)(2,1)S(1)}, bf16[512,256]{1,0:T(8,128)(2,1)S(1)}, u32[]{:S(2)}, u32[]{:S(2)}) collective-permute-start(bf16[512,256]{1,0:T(8,128)(2,1)S(1)} %shard_map.72.refs_0_), channel_id=1, source_target_pairs={{0,8},{8,0},{1,9},{9,1},{2,10},{10,2},{3,11},{11,3},{4,12},{12,4},... | collective-permute-start | bytes 786440 | tf_op jit(solution)/shard_map/ppermute | solution.py:404
  13.2 10.5 %collective-permute-start = (bf16[128,1024]{1,0:T(8,128)(2,1)S(1)}, bf16[128,1024]{1,0:T(8,128)(2,1)S(1)}, u32[]{:S(2)}, u32[]{:S(2)}) collective-permute-start(bf16[128,1024]{1,0:T(8,128)(2,1)S(1)} %shard_map.68), channel_id=1, source_target_pairs={{0,192},{64,128},{128,64},{192,0},{1,193},{65,129},{129,65},{193,1... | collective-permute-start | bytes 786440 | tf_op jit(solution)/shard_map/ppermute | solution.py:409
  16.3 12.6 %collective-permute-start.4 = (bf16[512,256]{1,0:T(8,128)(2,1)S(1)}, bf16[512,256]{1,0:T(8,128)(2,1)S(1)}, u32[]{:S(2)}, u32[]{:S(2)}) collective-permute-start(bf16[512,256]{1,0:T(8,128)(2,1)S(1)} %shard_map.72.refs_0_), channel_id=1, source_target_pairs={{0,192},{64,128},{128,64},{192,0},{1,193},{65,129},{129,65},{193,1... | collective-permute-start | bytes 786440 | tf_op jit(solution)/shard_map/ppermute | solution.py:409
  28.9 4.8 %collective-permute-start.6 = (bf16[512,256]{1,0:T(8,128)(2,1)S(1)}, bf16[512,256]{1,0:T(8,128)(2,1)S(1)}, u32[]{:S(2)}, u32[]{:S(2)}) collective-permute-start(bf16[512,256]{1,0:T(8,128)(2,1)S(1)} %collective-permute-done.4.refs_0_.refs_1_.refs_2_), channel_id=1, source_target_pairs={{0,8},{8,0},{1,9},{9,1},{2,10},{10,2},{3,11},{11,3},{4,12},{12,4},... | collective-permute-start | bytes 786440 | tf_op jit(solution)/shard_map/ppermute | solution.py:404
  28.9 11.7 %collective-permute-start.8 = (bf16[512,256]{1,0:T(8,128)(2,1)S(1)}, bf16[512,256]{1,0:T(8,128)(2,1)S(1)}, u32[]{:S(2)}, u32[]{:S(2)}) collective-permute-start(bf16[512,256]{1,0:T(8,128)(2,1)S(1)} %shard_map.72.refs_0_), channel_id=1, source_target_pairs={{0,128},{64,192},{128,0},{192,64},{1,129},{65,193},{129,1},{193,65... | collective-permute-start | bytes 786440 | tf_op jit(solution)/shard_map/ppermute | solution.py:404
  30.9 14.2 %collective-permute-start.7 = (bf16[512,256]{1,0:T(8,128)(2,1)S(1)}, bf16[512,256]{1,0:T(8,128)(2,1)S(1)}, u32[]{:S(2)}, u32[]{:S(2)}) collective-permute-start(bf16[512,256]{1,0:T(8,128)(2,1)S(1)} %shard_map.72.refs_0_), channel_id=1, source_target_pairs={{0,64},{64,0},{128,192},{192,128},{1,65},{65,1},{129,193},{193,129... | collective-permute-start | bytes 786440 | tf_op jit(solution)/shard_map/ppermute | solution.py:441
  52.3 11.2 %collective-permute-start.9 = (bf16[4096,256]{1,0:T(8,128)(2,1)S(1)}, bf16[4096,256]{1,0:T(8,128)(2,1)S(1)}, u32[]{:S(2)}, u32[]{:S(2)}) collective-permute-start(bf16[4096,256]{1,0:T(8,128)(2,1)S(1)} %shard_map.76.mine_ref), channel_id=1, source_target_pairs={{0,8},{8,0},{1,9},{9,1},{2,10},{10,2},{3,11},{11,3},{4,12},{12,4},... | collective-permute-start | bytes 6291464 | tf_op jit(solution)/shard_map/ppermute | solution.py:404
  52.4 4.5 %collective-permute-start.10 = (bf16[512,256]{1,0:T(8,128)(2,1)S(1)}, bf16[512,256]{1,0:T(8,128)(2,1)S(1)}, u32[]{:S(2)}, u32[]{:S(2)}) collective-permute-start(bf16[512,256]{1,0:T(8,128)(2,1)S(1)} %collective-permute-done.7.refs_2_.refs_4_), channel_id=1, source_target_pairs={{0,8},{8,0},{1,9},{9,1},{2,10},{10,2},{3,11},{11,3},{4,12},{12,4},... | collective-permute-start | bytes 786440 | tf_op jit(solution)/shard_map/ppermute | solution.py:404
  52.9 4.4 %collective-permute-start.11 = (bf16[512,256]{1,0:T(8,128)(2,1)S(1)}, bf16[512,256]{1,0:T(8,128)(2,1)S(1)}, u32[]{:S(2)}, u32[]{:S(2)}) collective-permute-start(bf16[512,256]{1,0:T(8,128)(2,1)S(1)} %collective-permute-done.8.refs_3_.refs_6_), channel_id=1, source_target_pairs={{0,8},{8,0},{1,9},{9,1},{2,10},{10,2},{3,11},{11,3},{4,12},{12,4},... | collective-permute-start | bytes 786440 | tf_op jit(solution)/shard_map/ppermute | solution.py:404
  64.1 28.2 %collective-permute-start.12 = (bf16[128,1024]{1,0:T(8,128)(2,1)S(1)}, bf16[128,1024]{1,0:T(8,128)(2,1)S(1)}, u32[]{:S(2)}, u32[]{:S(2)}) collective-permute-start(bf16[128,1024]{1,0:T(8,128)(2,1)S(1)} %get-tuple-element.51), channel_id=1, source_target_pairs={{0,192},{64,128},{128,64},{192,0},{1,193},{65,129},{129,65},{193,1... | collective-permute-start | bytes 786440 | tf_op jit(solution)/shard_map/ppermute | solution.py:409
  64.5 9.4 %collective-permute-start.13 = (f32[8,16]{1,0:T(8,128)S(1)}, f32[8,16]{1,0:T(8,128)S(1)}, u32[]{:S(2)}, u32[]{:S(2)}) collective-permute-start(f32[8,16]{1,0:T(8,128)S(1)} %get-tuple-element.55), channel_id=1, source_target_pairs={{0,192},{64,128},{128,64},{192,0},{1,193},{65,129},{129,65},{193,1... | collective-permute-start | bytes 1544 | tf_op jit(solution)/shard_map/ppermute | solution.py:409

commit v2 on v1

--- a/solution.py
+++ b/solution.py
@@ -366,7 +366,7 @@
         refs[-1][i * size : (i + 1) * size] = ref[...]
 
 
-def pack(at_ref, keys_ref, values_ref, kv_ref, sems):
+def pack(at_ref, place_ref, keys_ref, values_ref, kv_ref, sems):
     move(((keys_ref, kv_ref.at[:, :D]), (values_ref, kv_ref.at[:, D:])), sems)
 
 
@@ -378,6 +378,29 @@
     copy = pltpu.make_async_copy(back_ref, out_ref.at[:, back_ref.shape[1] :], sem)
     copy.start()
     copy.wait()
+
+
+def to_x(at_ref, a_ref, b_ref, *refs):
+    held = refs[-1]
+    held[...] = a_ref[...] + b_ref[...]
+    n = len(refs) - 1
+    rows = held.shape[0] // n
+    for k in range(n):
+        refs[k][...] = held[pl.ds(lax.rem(at_ref[0] + k, n) * rows, rows)]
+
+
+def to_w(at_ref, *refs):
+    parts, (keep_ref, send_ref, held) = refs[:-3], refs[-3:]
+    total = parts[0][...]
+    for ref in parts[1:]:
+        total = total + ref[...]
+    held[...] = total
+    keep_ref[...] = held[pl.ds(at_ref[1], 1)]
+    send_ref[...] = held[pl.ds(1 - at_ref[1], 1)]
+
+
+def add(a_ref, b_ref, out_ref):
+    out_ref[...] = a_ref[...] + b_ref[...]
 
 
 def call(kernel, outs, scratch, us, mib, *args, scalars=0, ins=None, spec=None, aliases=None):
@@ -415,6 +438,7 @@
     side = heads // 2
     depth = lax.axis_size("y")
     at = jnp.stack([lax.axis_index(a) for a in SEQ]).astype(jnp.int32)
+    place = jnp.stack([lax.axis_index(a) for a in ("x", "w")]).astype(jnp.int32)
     rows = side * tokens
     kv = call(
         pack,
@@ -423,9 +447,10 @@
         1,
         1,
         at,
+        place,
         pltpu.with_memory_space_constraint(keys, pltpu.HBM),
         pltpu.with_memory_space_constraint(values, pltpu.HBM),
-        ins=[SMEM] + [HBM] * 2,
+        ins=[SMEM] * 2 + [HBM] * 2,
     )
     zs = [shifted(kv, "z", k) for k in range(1, lax.axis_size("z"))]
     part = call(halve, shape((tokens, side * D), BF16), [], 0.2, 2, queries)
@@ -544,9 +569,34 @@
         acc,
         spec=(ANY, VMEM),
     )
-    loss = loss + loss_b
-    tiles = lax.all_to_all(loss[:, None, :], ("x", "w"), 0, 0, tiled=True)
-    token_loss = jnp.sum(tiles, axis=(0, 1))
+    width = tokens // parts
+    nx, nw = lax.axis_size("x"), lax.axis_size("w")
+    pieces = call(
+        to_x,
+        (shape((nw, width)),) * nx,
+        [pltpu.VMEM(grid, F32)],
+        0.1,
+        1,
+        place,
+        loss,
+        loss_b,
+        scalars=1,
+    )
+    parts_x = [pieces[0]]
+    for k in range(1, nx):
+        parts_x.append(shifted(pieces[k], "x", k))
+    keep, send = call(
+        to_w,
+        (shape((1, width)),) * 2,
+        [pltpu.VMEM((nw, width), F32)],
+        0.1,
+        1,
+        place,
+        *parts_x,
+        scalars=1,
+    )
+    got = mirrored(send, "w")
+    token_loss = call(add, shape((1, width)), [], 0.1, 1, keep, got).reshape(width)
     student = call(
         join,
         shape((tokens, heads * D), BF16),

time: 93.3 us -> 91.9 us (0.985)
  the two profiles are of different devices: /device:TPU:2 before, /device:TPU:6 now
where the time goes in v2:
time: 91.9 us; the launch traced here: 91.8 us
  Pallas kernels  35.3 us (38%)
  waiting for transfers between devices  30.5 us (33%)
  starting transfers between devices  24.9 us (27%)
  between operations  1 us (1%)
    pallas_call x16, Pallas kernels, call(): pl.pallas_call(kernel, out_shape=outs, in_specs=ins or [SMEM] * scalars +...  35.3 us
    ppermute x12, waiting for transfers between devices, shifted(): return lax.ppermute(x, axis, [(i, (i + k) % n) for i in range(n)])  13.1 us
    ppermute x5, waiting for transfers between devices, mirrored(): return lax.ppermute(x, axis, [(i, n - 1 - i) for i in range(n)])  13 us
    ppermute x5, starting transfers between devices, mirrored(): return lax.ppermute(x, axis, [(i, n - 1 - i) for i in range(n)])  11.9 us
    ppermute x12, starting transfers between devices, shifted(): return lax.ppermute(x, axis, [(i, (i + k) % n) for i in range(n)])  11.1 us
    ppermute x1, waiting for transfers between devices, body(): next_row = lax.ppermute(row, 'y', [(i, i ^ 1) for i in range(depth)])  4.4 us
    ppermute x1, starting transfers between devices, body(): next_row = lax.ppermute(row, 'y', [(i, i ^ 1) for i in range(depth)])  1.89 us
  transfers between devices with their start and end apart: 18, of which 12 were waited for; matrix products, arithmetic and copies ran while one was open for 0% of the time, Pallas kernels for 28%

profile of v2, /device:TPU:6, one launch (start us, length us, event | category | flops | bytes accessed | tf_op | source)
XLA Modules:
  0.0 91.8 jit_solution(12270606695025218895)
XLA Ops:
  0.8 1.3 %shard_map.69.refs_0_ = bf16[128,256]{1,0:T(8,128)(2,1)S(1)} custom-call(s32[3]{0:T(128)S(1)} %pad_add_fusion.at_ref, s32[2]{0:T(128)S(1)} %pad_add_fusion.1.place_ref.at_ref, bf16[128,128]{1,0:T(8,128)(2,1)} %keys_ref.1, bf16[128,128]{1,0:T(8,128)(2,1)} %values_ref.1), custom_call_target="tpu_custom_call" | custom-call | flops 1000000000 | bytes 1048576 | tf_op jit(solution)/shard_map/pallas_call | solution.py:407
  2.2 4.7 %collective-permute-start.3 = (bf16[128,256]{1,0:T(8,128)(2,1)S(1)}, bf16[128,256]{1,0:T(8,128)(2,1)S(1)}, u32[]{:S(2)}, u32[]{:S(2)}) collective-permute-start(bf16[128,256]{1,0:T(8,128)(2,1)S(1)} %shard_map.69.refs_0_), channel_id=1, source_target_pairs={{0,48},{16,0},{32,16},{48,32},{1,49},{17,1},{33,17},{49,33},{2,50}... | collective-permute-start | bytes 196616 | tf_op jit(solution)/shard_map/ppermute | solution.py:427
  7.5 1.0 %shard_map.71 = (bf16[1024,256]{1,0:T(8,128)(2,1)S(1)}, bf16[1024,256]{1,0:T(8,128)(2,1)S(1)}) custom-call(bf16[128,2048]{1,0:T(8,128)(2,1)S(1)} %copy-done, bf16[16,128,128]{2,1,0:T(8,128)(2,1)S(1)} %copy-done.2), custom_call_target="tpu_custom_call" | custom-call | flops 1500000000 | bytes 1048576 | tf_op jit(solution)/shard_map/pallas_call | solution.py:407
  9.3 3.8 %collective-permute-done.2.refs_2_ = bf16[128,256]{1,0:T(8,128)(2,1)S(1)} collective-permute-done((bf16[128,256]{1,0:T(8,128)(2,1)S(1)}, bf16[128,256]{1,0:T(8,128)(2,1)S(1)}, u32[]{:S(2)}, u32[]{:S(2)}) %collective-permute-start.2) | collective-permute-done | bytes 65568 | tf_op jit(solution)/shard_map/ppermute | solution.py:427
  13.3 3.1 %collective-permute-start = (bf16[128,1024]{1,0:T(8,128)(2,1)S(1)}, bf16[128,1024]{1,0:T(8,128)(2,1)S(1)}, u32[]{:S(2)}, u32[]{:S(2)}) collective-permute-start(bf16[128,1024]{1,0:T(8,128)(2,1)S(1)} %shard_map.68), channel_id=1, source_target_pairs={{0,192},{64,128},{128,64},{192,0},{1,193},{65,129},{129,65},{193,1... | collective-permute-start | bytes 786440 | tf_op jit(solution)/shard_map/ppermute | solution.py:432
  16.7 6.8 %shard_map.73 = (f32[1024,256]{1,0:T(8,128)S(1)}, f32[1024,128]{1,0:T(8,128)S(1)}, f32[1024,256]{1,0:T(8,128)S(1)}) custom-call(s32[3]{0:T(128)S(1)} %pad_add_fusion.at_ref, bf16[1024,256]{1,0:T(8,128)(2,1)S(1)} %get-tuple-element.40.q2_ref.q2a_ref, bf16[1024,256]{1,0:T(8,128)(2,1)S(1)} %get-tuple-element.41.qf_ref, bf16[2048,256]{1,0:T(8,128)(2,1)S(1)} %shard_map.70.wk_ref, ...), custom_call_target="tpu_custom_call" | custom-call | flops 6000000000 | bytes 1048576 | tf_op jit(solution)/shard_map/pallas_call | solution.py:407
  23.8 5.2 %collective-permute-done.4.refs_0_.refs_1_.refs_2_ = bf16[512,256]{1,0:T(8,128)(2,1)S(1)} collective-permute-done((bf16[512,256]{1,0:T(8,128)(2,1)S(1)}, bf16[512,256]{1,0:T(8,128)(2,1)S(1)}, u32[]{:S(2)}, u32[]{:S(2)}) %collective-permute-start.4) | collective-permute-done | bytes 262176 | tf_op jit(solution)/shard_map/ppermute | solution.py:432
  29.0 1.9 %collective-permute-start.8 = (bf16[512,256]{1,0:T(8,128)(2,1)S(1)}, bf16[512,256]{1,0:T(8,128)(2,1)S(1)}, u32[]{:S(2)}, u32[]{:S(2)}) collective-permute-start(bf16[512,256]{1,0:T(8,128)(2,1)S(1)} %shard_map.72.refs_0_), channel_id=1, source_target_pairs={{0,128},{64,192},{128,0},{192,64},{1,129},{65,193},{129,1},{193,65... | collective-permute-start | bytes 786440 | tf_op jit(solution)/shard_map/ppermute | solution.py:427
  30.9 1.9 %collective-permute-start.7 = (bf16[512,256]{1,0:T(8,128)(2,1)S(1)}, bf16[512,256]{1,0:T(8,128)(2,1)S(1)}, u32[]{:S(2)}, u32[]{:S(2)}) collective-permute-start(bf16[512,256]{1,0:T(8,128)(2,1)S(1)} %shard_map.72.refs_0_), channel_id=1, source_target_pairs={{0,64},{64,0},{128,192},{192,128},{1,65},{65,1},{129,193},{193,129... | collective-permute-start | bytes 786440 | tf_op jit(solution)/shard_map/ppermute | solution.py:466
  32.8 1.0 %shard_map.74 = (bf16[1024,256]{1,0:T(8,128)(2,1)S(1)}, bf16[1024,256]{1,0:T(8,128)(2,1)S(1)}) custom-call(bf16[128,1024]{1,0:T(8,128)(2,1)S(1)} %collective-permute-done.q_ref, bf16[16,128,128]{2,1,0:T(8,128)(2,1)S(1)} %copy-done.2), custom_call_target="tpu_custom_call" | custom-call | flops 1500000000 | bytes 1048576 | tf_op jit(solution)/shard_map/pallas_call | solution.py:407
  33.8 6.9 %shard_map.75 = (f32[1024,256]{1,0:T(8,128)S(1)}, f32[1024,128]{1,0:T(8,128)S(1)}, f32[1024,256]{1,0:T(8,128)S(1)}) custom-call(s32[3]{0:T(128)S(1)} %pad_add_fusion.at_ref, bf16[1024,256]{1,0:T(8,128)(2,1)S(1)} %get-tuple-element.46.q2_ref.q2b_ref, bf16[1024,256]{1,0:T(8,128)(2,1)S(1)} %get-tuple-element.45.qf_ref, bf16[2048,256]{1,0:T(8,128)(2,1)S(1)} %shard_map.70.wk_ref, ...), custom_call_target="tpu_custom_call" | custom-call | flops 6000000000 | bytes 1048576 | tf_op jit(solution)/shard_map/pallas_call | solution.py:407
  40.7 4.4 %collective-permute-done.7.refs_2_.refs_4_ = bf16[512,256]{1,0:T(8,128)(2,1)S(1)} collective-permute-done((bf16[512,256]{1,0:T(8,128)(2,1)S(1)}, bf16[512,256]{1,0:T(8,128)(2,1)S(1)}, u32[]{:S(2)}, u32[]{:S(2)}) %collective-permute-start.7) | collective-permute-done | bytes 262176 | tf_op jit(solution)/shard_map/ppermute | solution.py:466
  45.1 7.2 %shard_map.76.mine_ref = bf16[4096,256]{1,0:T(8,128)(2,1)S(1)} custom-call(s32[3]{0:T(128)S(1)} %pad_add_fusion.at_ref, bf16[2048,256]{1,0:T(8,128)(2,1)S(1)} %shard_map.70.wk_ref, bf16[512,256]{1,0:T(8,128)(2,1)S(1)} %shard_map.72.refs_0_, bf16[512,256]{1,0:T(8,128)(2,1)S(1)} %collective-permute-done.4.refs_0_.refs_1_.refs_2_, ...), custom_call_target="tpu_custom_call" | custom-call | flops 6000000000 | bytes 1048576 | tf_op jit(solution)/shard_map/pallas_call | solution.py:407
  53.1 3.9 %collective-permute-done.10.refs_5_ = bf16[512,256]{1,0:T(8,128)(2,1)S(1)} collective-permute-done((bf16[512,256]{1,0:T(8,128)(2,1)S(1)}, bf16[512,256]{1,0:T(8,128)(2,1)S(1)}, u32[]{:S(2)}, u32[]{:S(2)}) %collective-permute-start.10) | collective-permute-done | bytes 262176 | tf_op jit(solution)/shard_map/ppermute | solution.py:427
  57.4 6.1 %shard_map.77.acc_ref = f32[2048,256]{1,0:T(8,128)S(1)} custom-call(s32[3]{0:T(128)S(1)} %pad_add_fusion.at_ref, bf16[1024,256]{1,0:T(8,128)(2,1)S(1)} %get-tuple-element.40.q2_ref.q2a_ref, bf16[1024,256]{1,0:T(8,128)(2,1)S(1)} %get-tuple-element.46.q2_ref.q2b_ref, f32[1024,256]{1,0:T(8,128)S(1)} %get-tuple-element.53.acca_ref, ...), custom_call_target="tpu_custom_call" | custom-call | flops 6000000000 | bytes 1048576 | tf_op jit(solution)/shard_map/pallas_call | solution.py:407
  64.6 2.9 %collective-permute-start.13 = (f32[8,16]{1,0:T(8,128)S(1)}, f32[8,16]{1,0:T(8,128)S(1)}, u32[]{:S(2)}, u32[]{:S(2)}) collective-permute-start(f32[8,16]{1,0:T(8,128)S(1)} %get-tuple-element.61), channel_id=1, source_target_pairs={{0,192},{64,128},{128,64},{192,0},{1,193},{65,129},{129,65},{193,1... | collective-permute-start | bytes 1544 | tf_op jit(solution)/shard_map/ppermute | solution.py:432
  67.5 1.2 %shard_map.79 = (bf16[128,2048]{1,0:T(8,128)(2,1)}, f32[8,16]{1,0:T(8,128)S(1)}) custom-call(bf16[1024,256]{1,0:T(8,128)(2,1)S(1)} %get-tuple-element.41.qf_ref, f32[1024,256]{1,0:T(8,128)S(1)} %get-tuple-element.58.near_ref, bf16[4096,256]{1,0:T(8,128)(2,1)S(1)} %shard_map.76.mine_ref, bf16[4096,256]{1,0:T(8,128)(2,1)S(1)} %collective-permute-done.9.other_ref, ...), custom_call_target="tpu_custom_call" | custom-call | flops 1000000000 | bytes 1048576 | tf_op jit(solution)/shard_map/pallas_call | solution.py:407
  68.7 5.2 %collective-permute-done.13.b_ref = f32[8,16]{1,0:T(8,128)S(1)} collective-permute-done((f32[8,16]{1,0:T(8,128)S(1)}, f32[8,16]{1,0:T(8,128)S(1)}, u32[]{:S(2)}, u32[]{:S(2)}) %collective-permute-start.13) | collective-permute-done | bytes 544 | tf_op jit(solution)/shard_map/ppermute | solution.py:432
  75.0 2.4 %collective-permute-start.15 = (f32[2,16]{1,0:T(2,128)S(1)}, f32[2,16]{1,0:T(2,128)S(1)}, u32[]{:S(2)}, u32[]{:S(2)}) collective-permute-start(f32[2,16]{1,0:T(2,128)S(1)} %get-tuple-element.64), channel_id=1, source_target_pairs={{0,4},{2,6},{4,0},{6,2},{1,5},{3,7},{5,1},{7,3},{8,12},{10,14},{12... | collective-permute-start | bytes 392 | tf_op jit(solution)/shard_map/ppermute | solution.py:427
  78.1 2.0 %collective-permute-done.15.refs_2_ = f32[2,16]{1,0:T(2,128)S(1)} collective-permute-done((f32[2,16]{1,0:T(2,128)S(1)}, f32[2,16]{1,0:T(2,128)S(1)}, u32[]{:S(2)}, u32[]{:S(2)}) %collective-permute-start.15) | collective-permute-done | bytes 160 | tf_op jit(solution)/shard_map/ppermute | solution.py:427
  80.1 2.1 %collective-permute-done.16.refs_3_ = f32[2,16]{1,0:T(2,128)S(1)} collective-permute-done((f32[2,16]{1,0:T(2,128)S(1)}, f32[2,16]{1,0:T(2,128)S(1)}, u32[]{:S(2)}, u32[]{:S(2)}) %collective-permute-start.16) | collective-permute-done | bytes 160 | tf_op jit(solution)/shard_map/ppermute | solution.py:427
  82.8 5.3 %collective-permute-start.17 = (f32[1,16]{1,0:T(1,128)S(1)}, f32[1,16]{1,0:T(1,128)S(1)}, u32[]{:S(2)}, u32[]{:S(2)}) collective-permute-start(f32[1,16]{1,0:T(1,128)S(1)} %get-tuple-element.67), channel_id=1, source_target_pairs={{0,1},{1,0},{2,3},{3,2},{4,5},{5,4},{6,7},{7,6},{8,9},{9,8},{10,11... | collective-permute-start | bytes 200 | tf_op jit(solution)/shard_map/ppermute | solution.py:432
  88.1 2.3 %collective-permute-done.17.b_ref = f32[1,16]{1,0:T(1,128)S(1)} collective-permute-done((f32[1,16]{1,0:T(1,128)S(1)}, f32[1,16]{1,0:T(1,128)S(1)}, u32[]{:S(2)}, u32[]{:S(2)}) %collective-permute-start.17) | collective-permute-done | bytes 96 | tf_op jit(solution)/shard_map/ppermute | solution.py:432
  90.9 0.7 shard_map.80
  (36 shorter events, 7.3 us)
Async XLA Ops:
  0.6 6.9 %copy-start.2 = (bf16[16,128,128]{2,1,0:T(8,128)(2,1)S(1)}, bf16[16,128,128]{2,1,0:T(8,128)(2,1)}, u32[]{:S(2)}) copy-start(bf16[16,128,128]{2,1,0:T(8,128)(2,1)} %fq_ref.3) | copy-start | bytes 1572868
  0.6 6.9 %copy-start = (bf16[128,2048]{1,0:T(8,128)(2,1)S(1)}, bf16[128,2048]{1,0:T(8,128)(2,1)}, u32[]{:S(2)}) copy-start(bf16[128,2048]{1,0:T(8,128)(2,1)} %q_ref.3) | copy-start | bytes 1572868
  2.2 6.4 %copy-start.1 = (bf16[16,128,128]{2,1,0:T(8,128)(2,1)S(1)}, bf16[16,128,128]{2,1,0:T(8,128)(2,1)}, u32[]{:S(2)}) copy-start(bf16[16,128,128]{2,1,0:T(8,128)(2,1)} %fk_ref.1) | copy-start | bytes 1572868
  2.2 7.2 %collective-permute-start.3 = (bf16[128,256]{1,0:T(8,128)(2,1)S(1)}, bf16[128,256]{1,0:T(8,128)(2,1)S(1)}, u32[]{:S(2)}, u32[]{:S(2)}) collective-permute-start(bf16[128,256]{1,0:T(8,128)(2,1)S(1)} %shard_map.69.refs_0_), channel_id=1, source_target_pairs={{0,48},{16,0},{32,16},{48,32},{1,49},{17,1},{33,17},{49,33},{2,50}... | collective-permute-start | bytes 196616 | tf_op jit(solution)/shard_map/ppermute | solution.py:427
  6.9 6.3 %collective-permute-start.2 = (bf16[128,256]{1,0:T(8,128)(2,1)S(1)}, bf16[128,256]{1,0:T(8,128)(2,1)S(1)}, u32[]{:S(2)}, u32[]{:S(2)}) collective-permute-start(bf16[128,256]{1,0:T(8,128)(2,1)S(1)} %shard_map.69.refs_0_), channel_id=1, source_target_pairs={{0,32},{16,48},{32,0},{48,16},{1,33},{17,49},{33,1},{49,17},{2,34}... | collective-permute-start | bytes 196616 | tf_op jit(solution)/shard_map/ppermute | solution.py:427
  6.9 6.3 %collective-permute-start.1 = (bf16[128,256]{1,0:T(8,128)(2,1)S(1)}, bf16[128,256]{1,0:T(8,128)(2,1)S(1)}, u32[]{:S(2)}, u32[]{:S(2)}) collective-permute-start(bf16[128,256]{1,0:T(8,128)(2,1)S(1)} %shard_map.69.refs_0_), channel_id=1, source_target_pairs={{0,16},{16,32},{32,48},{48,0},{1,17},{17,33},{33,49},{49,1},{2,18}... | collective-permute-start | bytes 196616 | tf_op jit(solution)/shard_map/ppermute | solution.py:427
  13.2 3.5 %collective-permute-start.5 = (bf16[512,256]{1,0:T(8,128)(2,1)S(1)}, bf16[512,256]{1,0:T(8,128)(2,1)S(1)}, u32[]{:S(2)}, u32[]{:S(2)}) collective-permute-start(bf16[512,256]{1,0:T(8,128)(2,1)S(1)} %shard_map.72.refs_0_), channel_id=1, source_target_pairs={{0,8},{8,0},{1,9},{9,1},{2,10},{10,2},{3,11},{11,3},{4,12},{12,4},... | collective-permute-start | bytes 786440 | tf_op jit(solution)/shard_map/ppermute | solution.py:427
  13.3 10.5 %collective-permute-start = (bf16[128,1024]{1,0:T(8,128)(2,1)S(1)}, bf16[128,1024]{1,0:T(8,128)(2,1)S(1)}, u32[]{:S(2)}, u32[]{:S(2)}) collective-permute-start(bf16[128,1024]{1,0:T(8,128)(2,1)S(1)} %shard_map.68), channel_id=1, source_target_pairs={{0,192},{64,128},{128,64},{192,0},{1,193},{65,129},{129,65},{193,1... | collective-permute-start | bytes 786440 | tf_op jit(solution)/shard_map/ppermute | solution.py:432
  16.4 12.6 %collective-permute-start.4 = (bf16[512,256]{1,0:T(8,128)(2,1)S(1)}, bf16[512,256]{1,0:T(8,128)(2,1)S(1)}, u32[]{:S(2)}, u32[]{:S(2)}) collective-permute-start(bf16[512,256]{1,0:T(8,128)(2,1)S(1)} %shard_map.72.refs_0_), channel_id=1, source_target_pairs={{0,192},{64,128},{128,64},{192,0},{1,193},{65,129},{129,65},{193,1... | collective-permute-start | bytes 786440 | tf_op jit(solution)/shard_map/ppermute | solution.py:432
  29.0 4.8 %collective-permute-start.6 = (bf16[512,256]{1,0:T(8,128)(2,1)S(1)}, bf16[512,256]{1,0:T(8,128)(2,1)S(1)}, u32[]{:S(2)}, u32[]{:S(2)}) collective-permute-start(bf16[512,256]{1,0:T(8,128)(2,1)S(1)} %collective-permute-done.4.refs_0_.refs_1_.refs_2_), channel_id=1, source_target_pairs={{0,8},{8,0},{1,9},{9,1},{2,10},{10,2},{3,11},{11,3},{4,12},{12,4},... | collective-permute-start | bytes 786440 | tf_op jit(solution)/shard_map/ppermute | solution.py:427
  29.0 11.7 %collective-permute-start.8 = (bf16[512,256]{1,0:T(8,128)(2,1)S(1)}, bf16[512,256]{1,0:T(8,128)(2,1)S(1)}, u32[]{:S(2)}, u32[]{:S(2)}) collective-permute-start(bf16[512,256]{1,0:T(8,128)(2,1)S(1)} %shard_map.72.refs_0_), channel_id=1, source_target_pairs={{0,128},{64,192},{128,0},{192,64},{1,129},{65,193},{129,1},{193,65... | collective-permute-start | bytes 786440 | tf_op jit(solution)/shard_map/ppermute | solution.py:427
  30.9 14.2 %collective-permute-start.7 = (bf16[512,256]{1,0:T(8,128)(2,1)S(1)}, bf16[512,256]{1,0:T(8,128)(2,1)S(1)}, u32[]{:S(2)}, u32[]{:S(2)}) collective-permute-start(bf16[512,256]{1,0:T(8,128)(2,1)S(1)} %shard_map.72.refs_0_), channel_id=1, source_target_pairs={{0,64},{64,0},{128,192},{192,128},{1,65},{65,1},{129,193},{193,129... | collective-permute-start | bytes 786440 | tf_op jit(solution)/shard_map/ppermute | solution.py:466
  52.4 11.2 %collective-permute-start.9 = (bf16[4096,256]{1,0:T(8,128)(2,1)S(1)}, bf16[4096,256]{1,0:T(8,128)(2,1)S(1)}, u32[]{:S(2)}, u32[]{:S(2)}) collective-permute-start(bf16[4096,256]{1,0:T(8,128)(2,1)S(1)} %shard_map.76.mine_ref), channel_id=1, source_target_pairs={{0,8},{8,0},{1,9},{9,1},{2,10},{10,2},{3,11},{11,3},{4,12},{12,4},... | collective-permute-start | bytes 6291464 | tf_op jit(solution)/shard_map/ppermute | solution.py:427
  52.5 4.5 %collective-permute-start.10 = (bf16[512,256]{1,0:T(8,128)(2,1)S(1)}, bf16[512,256]{1,0:T(8,128)(2,1)S(1)}, u32[]{:S(2)}, u32[]{:S(2)}) collective-permute-start(bf16[512,256]{1,0:T(8,128)(2,1)S(1)} %collective-permute-done.7.refs_2_.refs_4_), channel_id=1, source_target_pairs={{0,8},{8,0},{1,9},{9,1},{2,10},{10,2},{3,11},{11,3},{4,12},{12,4},... | collective-permute-start | bytes 786440 | tf_op jit(solution)/shard_map/ppermute | solution.py:427
  53.0 4.4 %collective-permute-start.11 = (bf16[512,256]{1,0:T(8,128)(2,1)S(1)}, bf16[512,256]{1,0:T(8,128)(2,1)S(1)}, u32[]{:S(2)}, u32[]{:S(2)}) collective-permute-start(bf16[512,256]{1,0:T(8,128)(2,1)S(1)} %collective-permute-done.8.refs_3_.refs_6_), channel_id=1, source_target_pairs={{0,8},{8,0},{1,9},{9,1},{2,10},{10,2},{3,11},{11,3},{4,12},{12,4},... | collective-permute-start | bytes 786440 | tf_op jit(solution)/shard_map/ppermute | solution.py:427
  64.2 26.7 %collective-permute-start.12 = (bf16[128,1024]{1,0:T(8,128)(2,1)S(1)}, bf16[128,1024]{1,0:T(8,128)(2,1)S(1)}, u32[]{:S(2)}, u32[]{:S(2)}) collective-permute-start(bf16[128,1024]{1,0:T(8,128)(2,1)S(1)} %get-tuple-element.57), channel_id=1, source_target_pairs={{0,192},{64,128},{128,64},{192,0},{1,193},{65,129},{129,65},{193,1... | collective-permute-start | bytes 786440 | tf_op jit(solution)/shard_map/ppermute | solution.py:432
  64.6 9.4 %collective-permute-start.13 = (f32[8,16]{1,0:T(8,128)S(1)}, f32[8,16]{1,0:T(8,128)S(1)}, u32[]{:S(2)}, u32[]{:S(2)}) collective-permute-start(f32[8,16]{1,0:T(8,128)S(1)} %get-tuple-element.61), channel_id=1, source_target_pairs={{0,192},{64,128},{128,64},{192,0},{1,193},{65,129},{129,65},{193,1... | collective-permute-start | bytes 1544 | tf_op jit(solution)/shard_map/ppermute | solution.py:432
  74.5 3.7 %collective-permute-start.14 = (f32[2,16]{1,0:T(2,128)S(1)}, f32[2,16]{1,0:T(2,128)S(1)}, u32[]{:S(2)}, u32[]{:S(2)}) collective-permute-start(f32[2,16]{1,0:T(2,128)S(1)} %get-tuple-element.63), channel_id=1, source_target_pairs={{0,2},{2,4},{4,6},{6,0},{1,3},{3,5},{5,7},{7,1},{8,10},{10,12},{12... | collective-permute-start | bytes 392 | tf_op jit(solution)/shard_map/ppermute | solution.py:427
  75.0 5.1 %collective-permute-start.15 = (f32[2,16]{1,0:T(2,128)S(1)}, f32[2,16]{1,0:T(2,128)S(1)}, u32[]{:S(2)}, u32[]{:S(2)}) collective-permute-start(f32[2,16]{1,0:T(2,128)S(1)} %get-tuple-element.64), channel_id=1, source_target_pairs={{0,4},{2,6},{4,0},{6,2},{1,5},{3,7},{5,1},{7,3},{8,12},{10,14},{12... | collective-permute-start | bytes 392 | tf_op jit(solution)/shard_map/ppermute | solution.py:427
  77.5 4.8 %collective-permute-start.16 = (f32[2,16]{1,0:T(2,128)S(1)}, f32[2,16]{1,0:T(2,128)S(1)}, u32[]{:S(2)}, u32[]{:S(2)}) collective-permute-start(f32[2,16]{1,0:T(2,128)S(1)} %get-tuple-element.65), channel_id=1, source_target_pairs={{0,6},{2,0},{4,2},{6,4},{1,7},{3,1},{5,3},{7,5},{8,14},{10,8},{12,... | collective-permute-start | bytes 392 | tf_op jit(solution)/shard_map/ppermute | solution.py:427
  82.8 7.6 %collective-permute-start.17 = (f32[1,16]{1,0:T(1,128)S(1)}, f32[1,16]{1,0:T(1,128)S(1)}, u32[]{:S(2)}, u32[]{:S(2)}) collective-permute-start(f32[1,16]{1,0:T(1,128)S(1)} %get-tuple-element.67), channel_id=1, source_target_pairs={{0,1},{1,0},{2,3},{3,2},{4,5},{5,4},{6,7},{7,6},{8,9},{9,8},{10,11... | collective-permute-start | bytes 200 | tf_op jit(solution)/shard_map/ppermute | solution.py:432

commit v3 on v2

--- a/solution.py
+++ b/solution.py
@@ -25,6 +25,15 @@
 HBM = pl.BlockSpec(memory_space=pltpu.HBM)
 
 
+def place_of(at_ref, name):
+    sizes = {"w": 2, "x": 4, "c": 2, "z": 4, "y": 4}
+    below = 1
+    for axis, size in sizes.items():
+        if axis == name:
+            return lax.rem(lax.div(at_ref[0], below), size)
+        below *= size
+
+
 def mm(a, b):
     return jnp.dot(a, b, preferred_element_type=F32)
 
@@ -95,7 +104,7 @@
     many = s0.shape[0] // tokens
     groups = heads // many
     tile = wide // many
-    z, c = at_ref[1], at_ref[2]
+    z, c = place_of(at_ref, "z"), place_of(at_ref, "c")
     safe = jnp.broadcast_to(rows[0][:16, :D].astype(F32)[:1], (tokens, D))
     for side, ref in enumerate(rows):
         for slot in range(half // tokens):
@@ -178,7 +187,7 @@
 
 def absolute(at_ref, rows, store):
     depth = len(rows)
-    y = at_ref[0]
+    y = place_of(at_ref, "y")
     places = (y, depth - 1 - y, y + 1 - 2 * lax.rem(y, 2), lax.rem(y + depth // 2, depth))
     for r, refs in zip(places, rows):
 
@@ -196,8 +205,9 @@
 
 
 def unit_of(at_ref, u, half_heads):
-    mine = u < at_ref[0]
-    return jnp.where(mine, u, u - at_ref[0]), jnp.where(mine, 0, half_heads)
+    y = place_of(at_ref, "y")
+    mine = u < y
+    return jnp.where(mine, u, u - y), jnp.where(mine, 0, half_heads)
 
 
 def earlier_state(at_ref, wk_ref, *refs):
@@ -366,7 +376,7 @@
         refs[-1][i * size : (i + 1) * size] = ref[...]
 
 
-def pack(at_ref, place_ref, keys_ref, values_ref, kv_ref, sems):
+def pack(at_ref, keys_ref, values_ref, kv_ref, sems):
     move(((keys_ref, kv_ref.at[:, :D]), (values_ref, kv_ref.at[:, D:])), sems)
 
 
@@ -386,7 +396,7 @@
     n = len(refs) - 1
     rows = held.shape[0] // n
     for k in range(n):
-        refs[k][...] = held[pl.ds(lax.rem(at_ref[0] + k, n) * rows, rows)]
+        refs[k][...] = held[pl.ds(lax.rem(place_of(at_ref, "x") + k, n) * rows, rows)]
 
 
 def to_w(at_ref, *refs):
@@ -395,8 +405,9 @@
     for ref in parts[1:]:
         total = total + ref[...]
     held[...] = total
-    keep_ref[...] = held[pl.ds(at_ref[1], 1)]
-    send_ref[...] = held[pl.ds(1 - at_ref[1], 1)]
+    w = place_of(at_ref, "w")
+    keep_ref[...] = held[pl.ds(w, 1)]
+    send_ref[...] = held[pl.ds(1 - w, 1)]
 
 
 def add(a_ref, b_ref, out_ref):
@@ -437,8 +448,7 @@
     heads = feat_q.shape[0]
     side = heads // 2
     depth = lax.axis_size("y")
-    at = jnp.stack([lax.axis_index(a) for a in SEQ]).astype(jnp.int32)
-    place = jnp.stack([lax.axis_index(a) for a in ("x", "w")]).astype(jnp.int32)
+    at = lax.axis_index((*SEQ, "x", "w")).astype(jnp.int32).reshape(1)
     rows = side * tokens
     kv = call(
         pack,
@@ -447,10 +457,9 @@
         1,
         1,
         at,
-        place,
         pltpu.with_memory_space_constraint(keys, pltpu.HBM),
         pltpu.with_memory_space_constraint(values, pltpu.HBM),
-        ins=[SMEM] * 2 + [HBM] * 2,
+        ins=[SMEM] + [HBM] * 2,
     )
     zs = [shifted(kv, "z", k) for k in range(1, lax.axis_size("z"))]
     part = call(halve, shape((tokens, side * D), BF16), [], 0.2, 2, queries)
@@ -577,7 +586,7 @@
         [pltpu.VMEM(grid, F32)],
         0.1,
         1,
-        place,
+        at,
         loss,
         loss_b,
         scalars=1,
@@ -591,7 +600,7 @@
         [pltpu.VMEM((nw, width), F32)],
         0.1,
         1,
-        place,
+        at,
         *parts_x,
         scalars=1,
     )

time: 91.9 us -> 89 us (0.968)
  Pallas kernels: 35.3 us -> 31.6 us
  waiting for transfers between devices: 30.5 us -> 31.6 us
    pallas_call x16, Pallas kernels: 35.3 us -> 31.6 us  [call(): pl.pallas_call(kernel, out_shape=outs, in_specs=ins or [SMEM] * scalars +...]
  transfers between devices with their start and end apart: 18 -> 18, of which waited for: 12 -> 12; matrix products, arithmetic and copies ran while one was open for 0% -> 0% of each run, Pallas kernels for 28% -> 25%
where the time goes in v3:
time: 89 us; the launch traced here: 88.9 us
  Pallas kernels  31.6 us (36%)
  waiting for transfers between devices  31.6 us (36%)
  starting transfers between devices  24.8 us (28%)
  between operations  0.99 us (1%)
    pallas_call x16, Pallas kernels, call(): pl.pallas_call(kernel, out_shape=outs, in_specs=ins or [SMEM] * scalars +...  31.6 us
    ppermute x5, waiting for transfers between devices, mirrored(): return lax.ppermute(x, axis, [(i, n - 1 - i) for i in range(n)])  13.5 us
    ppermute x12, waiting for transfers between devices, shifted(): return lax.ppermute(x, axis, [(i, (i + k) % n) for i in range(n)])  13.1 us
    ppermute x5, starting transfers between devices, mirrored(): return lax.ppermute(x, axis, [(i, n - 1 - i) for i in range(n)])  11.8 us
    ppermute x12, starting transfers between devices, shifted(): return lax.ppermute(x, axis, [(i, (i + k) % n) for i in range(n)])  11.1 us
    ppermute x1, waiting for transfers between devices, body(): next_row = lax.ppermute(row, 'y', [(i, i ^ 1) for i in range(depth)])  4.95 us
    ppermute x1, starting transfers between devices, body(): next_row = lax.ppermute(row, 'y', [(i, i ^ 1) for i in range(depth)])  1.89 us
  transfers between devices with their start and end apart: 18, of which 12 were waited for; matrix products, arithmetic and copies ran while one was open for 0% of the time, Pallas kernels for 25%

profile of v3, /device:TPU:6, one launch (start us, length us, event | category | flops | bytes accessed | tf_op | source)
XLA Modules:
  0.0 88.9 jit_solution(1196573969622249788)
XLA Ops:
  0.7 0.9 shard_map.69.refs_0_
  1.6 4.7 %collective-permute-start.3 = (bf16[128,256]{1,0:T(8,128)(2,1)S(1)}, bf16[128,256]{1,0:T(8,128)(2,1)S(1)}, u32[]{:S(2)}, u32[]{:S(2)}) collective-permute-start(bf16[128,256]{1,0:T(8,128)(2,1)S(1)} %shard_map.69.refs_0_), channel_id=1, source_target_pairs={{0,48},{16,0},{32,16},{48,32},{1,49},{17,1},{33,17},{49,33},{2,50}... | collective-permute-start | bytes 196616 | tf_op jit(solution)/shard_map/ppermute | solution.py:438
  6.9 1.0 %shard_map.71 = (bf16[1024,256]{1,0:T(8,128)(2,1)S(1)}, bf16[1024,256]{1,0:T(8,128)(2,1)S(1)}) custom-call(bf16[128,2048]{1,0:T(8,128)(2,1)S(1)} %copy-done, bf16[16,128,128]{2,1,0:T(8,128)(2,1)S(1)} %copy-done.2), custom_call_target="tpu_custom_call" | custom-call | flops 1500000000 | bytes 1048576 | tf_op jit(solution)/shard_map/pallas_call | solution.py:418
  8.7 3.8 %collective-permute-done.2.refs_2_ = bf16[128,256]{1,0:T(8,128)(2,1)S(1)} collective-permute-done((bf16[128,256]{1,0:T(8,128)(2,1)S(1)}, bf16[128,256]{1,0:T(8,128)(2,1)S(1)}, u32[]{:S(2)}, u32[]{:S(2)}) %collective-permute-start.2) | collective-permute-done | bytes 65568 | tf_op jit(solution)/shard_map/ppermute | solution.py:438
  12.7 3.1 %collective-permute-start = (bf16[128,1024]{1,0:T(8,128)(2,1)S(1)}, bf16[128,1024]{1,0:T(8,128)(2,1)S(1)}, u32[]{:S(2)}, u32[]{:S(2)}) collective-permute-start(bf16[128,1024]{1,0:T(8,128)(2,1)S(1)} %shard_map.68), channel_id=1, source_target_pairs={{0,192},{64,128},{128,64},{192,0},{1,193},{65,129},{129,65},{193,1... | collective-permute-start | bytes 786440 | tf_op jit(solution)/shard_map/ppermute | solution.py:443
  16.0 6.3 %shard_map.73 = (f32[1024,256]{1,0:T(8,128)S(1)}, f32[1024,128]{1,0:T(8,128)S(1)}, f32[1024,256]{1,0:T(8,128)S(1)}) custom-call(s32[1]{0:T(128)} %bitcast.at_ref, bf16[1024,256]{1,0:T(8,128)(2,1)S(1)} %get-tuple-element.40.q2_ref.q2a_ref, bf16[1024,256]{1,0:T(8,128)(2,1)S(1)} %get-tuple-element.41.qf_ref, bf16[2048,256]{1,0:T(8,128)(2,1)S(1)} %shard_map.70.wk_ref, ...), custom_call_target="tpu_custom_call" | custom-call | flops 6000000000 | bytes 1048576 | tf_op jit(solution)/shard_map/pallas_call | solution.py:418
  22.3 0.9 collective-permute-done.q_ref
  23.2 5.2 %collective-permute-done.4.refs_0_.refs_1_.refs_2_ = bf16[512,256]{1,0:T(8,128)(2,1)S(1)} collective-permute-done((bf16[512,256]{1,0:T(8,128)(2,1)S(1)}, bf16[512,256]{1,0:T(8,128)(2,1)S(1)}, u32[]{:S(2)}, u32[]{:S(2)}) %collective-permute-start.4) | collective-permute-done | bytes 262176 | tf_op jit(solution)/shard_map/ppermute | solution.py:443
  28.4 1.9 %collective-permute-start.8 = (bf16[512,256]{1,0:T(8,128)(2,1)S(1)}, bf16[512,256]{1,0:T(8,128)(2,1)S(1)}, u32[]{:S(2)}, u32[]{:S(2)}) collective-permute-start(bf16[512,256]{1,0:T(8,128)(2,1)S(1)} %shard_map.72.refs_0_), channel_id=1, source_target_pairs={{0,128},{64,192},{128,0},{192,64},{1,129},{65,193},{129,1},{193,65... | collective-permute-start | bytes 786440 | tf_op jit(solution)/shard_map/ppermute | solution.py:438
  30.3 1.9 %collective-permute-start.7 = (bf16[512,256]{1,0:T(8,128)(2,1)S(1)}, bf16[512,256]{1,0:T(8,128)(2,1)S(1)}, u32[]{:S(2)}, u32[]{:S(2)}) collective-permute-start(bf16[512,256]{1,0:T(8,128)(2,1)S(1)} %shard_map.72.refs_0_), channel_id=1, source_target_pairs={{0,64},{64,0},{128,192},{192,128},{1,65},{65,1},{129,193},{193,129... | collective-permute-start | bytes 786440 | tf_op jit(solution)/shard_map/ppermute | solution.py:475
  32.2 1.0 %shard_map.74 = (bf16[1024,256]{1,0:T(8,128)(2,1)S(1)}, bf16[1024,256]{1,0:T(8,128)(2,1)S(1)}) custom-call(bf16[128,1024]{1,0:T(8,128)(2,1)S(1)} %collective-permute-done.q_ref, bf16[16,128,128]{2,1,0:T(8,128)(2,1)S(1)} %copy-done.2), custom_call_target="tpu_custom_call" | custom-call | flops 1500000000 | bytes 1048576 | tf_op jit(solution)/shard_map/pallas_call | solution.py:418
  33.2 6.3 %shard_map.75 = (f32[1024,256]{1,0:T(8,128)S(1)}, f32[1024,128]{1,0:T(8,128)S(1)}, f32[1024,256]{1,0:T(8,128)S(1)}) custom-call(s32[1]{0:T(128)} %bitcast.at_ref, bf16[1024,256]{1,0:T(8,128)(2,1)S(1)} %get-tuple-element.46.q2_ref.q2b_ref, bf16[1024,256]{1,0:T(8,128)(2,1)S(1)} %get-tuple-element.45.qf_ref, bf16[2048,256]{1,0:T(8,128)(2,1)S(1)} %shard_map.70.wk_ref, ...), custom_call_target="tpu_custom_call" | custom-call | flops 6000000000 | bytes 1048576 | tf_op jit(solution)/shard_map/pallas_call | solution.py:418
  39.6 4.9 %collective-permute-done.7.refs_2_.refs_4_ = bf16[512,256]{1,0:T(8,128)(2,1)S(1)} collective-permute-done((bf16[512,256]{1,0:T(8,128)(2,1)S(1)}, bf16[512,256]{1,0:T(8,128)(2,1)S(1)}, u32[]{:S(2)}, u32[]{:S(2)}) %collective-permute-start.7) | collective-permute-done | bytes 262176 | tf_op jit(solution)/shard_map/ppermute | solution.py:475
  44.5 6.7 %shard_map.76.mine_ref = bf16[4096,256]{1,0:T(8,128)(2,1)S(1)} custom-call(s32[1]{0:T(128)} %bitcast.at_ref, bf16[2048,256]{1,0:T(8,128)(2,1)S(1)} %shard_map.70.wk_ref, bf16[512,256]{1,0:T(8,128)(2,1)S(1)} %shard_map.72.refs_0_, bf16[512,256]{1,0:T(8,128)(2,1)S(1)} %collective-permute-done.4.refs_0_.refs_1_.refs_2_, ...), custom_call_target="tpu_custom_call" | custom-call | flops 6000000000 | bytes 1048576 | tf_op jit(solution)/shard_map/pallas_call | solution.py:418
  51.9 3.9 %collective-permute-done.10.refs_5_ = bf16[512,256]{1,0:T(8,128)(2,1)S(1)} collective-permute-done((bf16[512,256]{1,0:T(8,128)(2,1)S(1)}, bf16[512,256]{1,0:T(8,128)(2,1)S(1)}, u32[]{:S(2)}, u32[]{:S(2)}) %collective-permute-start.10) | collective-permute-done | bytes 262176 | tf_op jit(solution)/shard_map/ppermute | solution.py:438
  56.2 5.6 %shard_map.77.acc_ref = f32[2048,256]{1,0:T(8,128)S(1)} custom-call(s32[1]{0:T(128)} %bitcast.at_ref, bf16[1024,256]{1,0:T(8,128)(2,1)S(1)} %get-tuple-element.40.q2_ref.q2a_ref, bf16[1024,256]{1,0:T(8,128)(2,1)S(1)} %get-tuple-element.46.q2_ref.q2b_ref, f32[1024,256]{1,0:T(8,128)S(1)} %get-tuple-element.53.acca_ref, ...), custom_call_target="tpu_custom_call" | custom-call | flops 6000000000 | bytes 1048576 | tf_op jit(solution)/shard_map/pallas_call | solution.py:418
  62.9 2.9 %collective-permute-start.13 = (f32[8,16]{1,0:T(8,128)S(1)}, f32[8,16]{1,0:T(8,128)S(1)}, u32[]{:S(2)}, u32[]{:S(2)}) collective-permute-start(f32[8,16]{1,0:T(8,128)S(1)} %get-tuple-element.61), channel_id=1, source_target_pairs={{0,192},{64,128},{128,64},{192,0},{1,193},{65,129},{129,65},{193,1... | collective-permute-start | bytes 1544 | tf_op jit(solution)/shard_map/ppermute | solution.py:443
  65.8 1.2 %shard_map.79 = (bf16[128,2048]{1,0:T(8,128)(2,1)}, f32[8,16]{1,0:T(8,128)S(1)}) custom-call(bf16[1024,256]{1,0:T(8,128)(2,1)S(1)} %get-tuple-element.41.qf_ref, f32[1024,256]{1,0:T(8,128)S(1)} %get-tuple-element.58.near_ref, bf16[4096,256]{1,0:T(8,128)(2,1)S(1)} %shard_map.76.mine_ref, bf16[4096,256]{1,0:T(8,128)(2,1)S(1)} %collective-permute-done.9.other_ref, ...), custom_call_target="tpu_custom_call" | custom-call | flops 1000000000 | bytes 1048576 | tf_op jit(solution)/shard_map/pallas_call | solution.py:418
  67.0 5.2 %collective-permute-done.13.b_ref = f32[8,16]{1,0:T(8,128)S(1)} collective-permute-done((f32[8,16]{1,0:T(8,128)S(1)}, f32[8,16]{1,0:T(8,128)S(1)}, u32[]{:S(2)}, u32[]{:S(2)}) %collective-permute-start.13) | collective-permute-done | bytes 544 | tf_op jit(solution)/shard_map/ppermute | solution.py:443
  72.8 2.4 %collective-permute-start.15 = (f32[2,16]{1,0:T(2,128)S(1)}, f32[2,16]{1,0:T(2,128)S(1)}, u32[]{:S(2)}, u32[]{:S(2)}) collective-permute-start(f32[2,16]{1,0:T(2,128)S(1)} %get-tuple-element.64), channel_id=1, source_target_pairs={{0,4},{2,6},{4,0},{6,2},{1,5},{3,7},{5,1},{7,3},{8,12},{10,14},{12... | collective-permute-start | bytes 392 | tf_op jit(solution)/shard_map/ppermute | solution.py:438
  75.9 2.0 %collective-permute-done.15.refs_2_ = f32[2,16]{1,0:T(2,128)S(1)} collective-permute-done((f32[2,16]{1,0:T(2,128)S(1)}, f32[2,16]{1,0:T(2,128)S(1)}, u32[]{:S(2)}, u32[]{:S(2)}) %collective-permute-start.15) | collective-permute-done | bytes 160 | tf_op jit(solution)/shard_map/ppermute | solution.py:438
  77.9 2.1 %collective-permute-done.16.refs_3_ = f32[2,16]{1,0:T(2,128)S(1)} collective-permute-done((f32[2,16]{1,0:T(2,128)S(1)}, f32[2,16]{1,0:T(2,128)S(1)}, u32[]{:S(2)}, u32[]{:S(2)}) %collective-permute-start.16) | collective-permute-done | bytes 160 | tf_op jit(solution)/shard_map/ppermute | solution.py:438
  80.0 5.2 %collective-permute-start.17 = (f32[1,16]{1,0:T(1,128)S(1)}, f32[1,16]{1,0:T(1,128)S(1)}, u32[]{:S(2)}, u32[]{:S(2)}) collective-permute-start(f32[1,16]{1,0:T(1,128)S(1)} %get-tuple-element.67), channel_id=1, source_target_pairs={{0,1},{1,0},{2,3},{3,2},{4,5},{5,4},{6,7},{7,6},{8,9},{9,8},{10,11... | collective-permute-start | bytes 200 | tf_op jit(solution)/shard_map/ppermute | solution.py:443
  85.3 2.3 %collective-permute-done.17.b_ref = f32[1,16]{1,0:T(1,128)S(1)} collective-permute-done((f32[1,16]{1,0:T(1,128)S(1)}, f32[1,16]{1,0:T(1,128)S(1)}, u32[]{:S(2)}, u32[]{:S(2)}) %collective-permute-start.17) | collective-permute-done | bytes 96 | tf_op jit(solution)/shard_map/ppermute | solution.py:443
  (34 shorter events, 6.4 us)
Async XLA Ops:
  0.6 6.3 %copy-start.2 = (bf16[16,128,128]{2,1,0:T(8,128)(2,1)S(1)}, bf16[16,128,128]{2,1,0:T(8,128)(2,1)}, u32[]{:S(2)}) copy-start(bf16[16,128,128]{2,1,0:T(8,128)(2,1)} %fq_ref.3) | copy-start | bytes 1572868
  0.6 6.3 %copy-start = (bf16[128,2048]{1,0:T(8,128)(2,1)S(1)}, bf16[128,2048]{1,0:T(8,128)(2,1)}, u32[]{:S(2)}) copy-start(bf16[128,2048]{1,0:T(8,128)(2,1)} %q_ref.3) | copy-start | bytes 1572868
  1.5 6.4 %copy-start.1 = (bf16[16,128,128]{2,1,0:T(8,128)(2,1)S(1)}, bf16[16,128,128]{2,1,0:T(8,128)(2,1)}, u32[]{:S(2)}) copy-start(bf16[16,128,128]{2,1,0:T(8,128)(2,1)} %fk_ref.1) | copy-start | bytes 1572868
  1.6 7.2 %collective-permute-start.3 = (bf16[128,256]{1,0:T(8,128)(2,1)S(1)}, bf16[128,256]{1,0:T(8,128)(2,1)S(1)}, u32[]{:S(2)}, u32[]{:S(2)}) collective-permute-start(bf16[128,256]{1,0:T(8,128)(2,1)S(1)} %shard_map.69.refs_0_), channel_id=1, source_target_pairs={{0,48},{16,0},{32,16},{48,32},{1,49},{17,1},{33,17},{49,33},{2,50}... | collective-permute-start | bytes 196616 | tf_op jit(solution)/shard_map/ppermute | solution.py:438
  6.3 6.3 %collective-permute-start.2 = (bf16[128,256]{1,0:T(8,128)(2,1)S(1)}, bf16[128,256]{1,0:T(8,128)(2,1)S(1)}, u32[]{:S(2)}, u32[]{:S(2)}) collective-permute-start(bf16[128,256]{1,0:T(8,128)(2,1)S(1)} %shard_map.69.refs_0_), channel_id=1, source_target_pairs={{0,32},{16,48},{32,0},{48,16},{1,33},{17,49},{33,1},{49,17},{2,34}... | collective-permute-start | bytes 196616 | tf_op jit(solution)/shard_map/ppermute | solution.py:438
  6.3 6.3 %collective-permute-start.1 = (bf16[128,256]{1,0:T(8,128)(2,1)S(1)}, bf16[128,256]{1,0:T(8,128)(2,1)S(1)}, u32[]{:S(2)}, u32[]{:S(2)}) collective-permute-start(bf16[128,256]{1,0:T(8,128)(2,1)S(1)} %shard_map.69.refs_0_), channel_id=1, source_target_pairs={{0,16},{16,32},{32,48},{48,0},{1,17},{17,33},{33,49},{49,1},{2,18}... | collective-permute-start | bytes 196616 | tf_op jit(solution)/shard_map/ppermute | solution.py:438
  12.6 3.5 %collective-permute-start.5 = (bf16[512,256]{1,0:T(8,128)(2,1)S(1)}, bf16[512,256]{1,0:T(8,128)(2,1)S(1)}, u32[]{:S(2)}, u32[]{:S(2)}) collective-permute-start(bf16[512,256]{1,0:T(8,128)(2,1)S(1)} %shard_map.72.refs_0_), channel_id=1, source_target_pairs={{0,8},{8,0},{1,9},{9,1},{2,10},{10,2},{3,11},{11,3},{4,12},{12,4},... | collective-permute-start | bytes 786440 | tf_op jit(solution)/shard_map/ppermute | solution.py:438
  12.7 10.5 %collective-permute-start = (bf16[128,1024]{1,0:T(8,128)(2,1)S(1)}, bf16[128,1024]{1,0:T(8,128)(2,1)S(1)}, u32[]{:S(2)}, u32[]{:S(2)}) collective-permute-start(bf16[128,1024]{1,0:T(8,128)(2,1)S(1)} %shard_map.68), channel_id=1, source_target_pairs={{0,192},{64,128},{128,64},{192,0},{1,193},{65,129},{129,65},{193,1... | collective-permute-start | bytes 786440 | tf_op jit(solution)/shard_map/ppermute | solution.py:443
  15.8 12.6 %collective-permute-start.4 = (bf16[512,256]{1,0:T(8,128)(2,1)S(1)}, bf16[512,256]{1,0:T(8,128)(2,1)S(1)}, u32[]{:S(2)}, u32[]{:S(2)}) collective-permute-start(bf16[512,256]{1,0:T(8,128)(2,1)S(1)} %shard_map.72.refs_0_), channel_id=1, source_target_pairs={{0,192},{64,128},{128,64},{192,0},{1,193},{65,129},{129,65},{193,1... | collective-permute-start | bytes 786440 | tf_op jit(solution)/shard_map/ppermute | solution.py:443
  28.4 4.8 %collective-permute-start.6 = (bf16[512,256]{1,0:T(8,128)(2,1)S(1)}, bf16[512,256]{1,0:T(8,128)(2,1)S(1)}, u32[]{:S(2)}, u32[]{:S(2)}) collective-permute-start(bf16[512,256]{1,0:T(8,128)(2,1)S(1)} %collective-permute-done.4.refs_0_.refs_1_.refs_2_), channel_id=1, source_target_pairs={{0,8},{8,0},{1,9},{9,1},{2,10},{10,2},{3,11},{11,3},{4,12},{12,4},... | collective-permute-start | bytes 786440 | tf_op jit(solution)/shard_map/ppermute | solution.py:438
  28.4 11.2 %collective-permute-start.8 = (bf16[512,256]{1,0:T(8,128)(2,1)S(1)}, bf16[512,256]{1,0:T(8,128)(2,1)S(1)}, u32[]{:S(2)}, u32[]{:S(2)}) collective-permute-start(bf16[512,256]{1,0:T(8,128)(2,1)S(1)} %shard_map.72.refs_0_), channel_id=1, source_target_pairs={{0,128},{64,192},{128,0},{192,64},{1,129},{65,193},{129,1},{193,65... | collective-permute-start | bytes 786440 | tf_op jit(solution)/shard_map/ppermute | solution.py:438
  30.3 14.2 %collective-permute-start.7 = (bf16[512,256]{1,0:T(8,128)(2,1)S(1)}, bf16[512,256]{1,0:T(8,128)(2,1)S(1)}, u32[]{:S(2)}, u32[]{:S(2)}) collective-permute-start(bf16[512,256]{1,0:T(8,128)(2,1)S(1)} %shard_map.72.refs_0_), channel_id=1, source_target_pairs={{0,64},{64,0},{128,192},{192,128},{1,65},{65,1},{129,193},{193,129... | collective-permute-start | bytes 786440 | tf_op jit(solution)/shard_map/ppermute | solution.py:475
  51.2 10.6 %collective-permute-start.9 = (bf16[4096,256]{1,0:T(8,128)(2,1)S(1)}, bf16[4096,256]{1,0:T(8,128)(2,1)S(1)}, u32[]{:S(2)}, u32[]{:S(2)}) collective-permute-start(bf16[4096,256]{1,0:T(8,128)(2,1)S(1)} %shard_map.76.mine_ref), channel_id=1, source_target_pairs={{0,8},{8,0},{1,9},{9,1},{2,10},{10,2},{3,11},{11,3},{4,12},{12,4},... | collective-permute-start | bytes 6291464 | tf_op jit(solution)/shard_map/ppermute | solution.py:438
  51.3 4.5 %collective-permute-start.10 = (bf16[512,256]{1,0:T(8,128)(2,1)S(1)}, bf16[512,256]{1,0:T(8,128)(2,1)S(1)}, u32[]{:S(2)}, u32[]{:S(2)}) collective-permute-start(bf16[512,256]{1,0:T(8,128)(2,1)S(1)} %collective-permute-done.7.refs_2_.refs_4_), channel_id=1, source_target_pairs={{0,8},{8,0},{1,9},{9,1},{2,10},{10,2},{3,11},{11,3},{4,12},{12,4},... | collective-permute-start | bytes 786440 | tf_op jit(solution)/shard_map/ppermute | solution.py:438
  51.8 4.4 %collective-permute-start.11 = (bf16[512,256]{1,0:T(8,128)(2,1)S(1)}, bf16[512,256]{1,0:T(8,128)(2,1)S(1)}, u32[]{:S(2)}, u32[]{:S(2)}) collective-permute-start(bf16[512,256]{1,0:T(8,128)(2,1)S(1)} %collective-permute-done.8.refs_3_.refs_6_), channel_id=1, source_target_pairs={{0,8},{8,0},{1,9},{9,1},{2,10},{10,2},{3,11},{11,3},{4,12},{12,4},... | collective-permute-start | bytes 786440 | tf_op jit(solution)/shard_map/ppermute | solution.py:438
  62.5 25.5 %collective-permute-start.12 = (bf16[128,1024]{1,0:T(8,128)(2,1)S(1)}, bf16[128,1024]{1,0:T(8,128)(2,1)S(1)}, u32[]{:S(2)}, u32[]{:S(2)}) collective-permute-start(bf16[128,1024]{1,0:T(8,128)(2,1)S(1)} %get-tuple-element.57), channel_id=1, source_target_pairs={{0,192},{64,128},{128,64},{192,0},{1,193},{65,129},{129,65},{193,1... | collective-permute-start | bytes 786440 | tf_op jit(solution)/shard_map/ppermute | solution.py:443
  62.9 9.3 %collective-permute-start.13 = (f32[8,16]{1,0:T(8,128)S(1)}, f32[8,16]{1,0:T(8,128)S(1)}, u32[]{:S(2)}, u32[]{:S(2)}) collective-permute-start(f32[8,16]{1,0:T(8,128)S(1)} %get-tuple-element.61), channel_id=1, source_target_pairs={{0,192},{64,128},{128,64},{192,0},{1,193},{65,129},{129,65},{193,1... | collective-permute-start | bytes 1544 | tf_op jit(solution)/shard_map/ppermute | solution.py:443
  72.3 3.6 %collective-permute-start.14 = (f32[2,16]{1,0:T(2,128)S(1)}, f32[2,16]{1,0:T(2,128)S(1)}, u32[]{:S(2)}, u32[]{:S(2)}) collective-permute-start(f32[2,16]{1,0:T(2,128)S(1)} %get-tuple-element.63), channel_id=1, source_target_pairs={{0,2},{2,4},{4,6},{6,0},{1,3},{3,5},{5,7},{7,1},{8,10},{10,12},{12... | collective-permute-start | bytes 392 | tf_op jit(solution)/shard_map/ppermute | solution.py:438
  72.8 5.1 %collective-permute-start.15 = (f32[2,16]{1,0:T(2,128)S(1)}, f32[2,16]{1,0:T(2,128)S(1)}, u32[]{:S(2)}, u32[]{:S(2)}) collective-permute-start(f32[2,16]{1,0:T(2,128)S(1)} %get-tuple-element.64), channel_id=1, source_target_pairs={{0,4},{2,6},{4,0},{6,2},{1,5},{3,7},{5,1},{7,3},{8,12},{10,14},{12... | collective-permute-start | bytes 392 | tf_op jit(solution)/shard_map/ppermute | solution.py:438
  75.2 4.8 %collective-permute-start.16 = (f32[2,16]{1,0:T(2,128)S(1)}, f32[2,16]{1,0:T(2,128)S(1)}, u32[]{:S(2)}, u32[]{:S(2)}) collective-permute-start(f32[2,16]{1,0:T(2,128)S(1)} %get-tuple-element.65), channel_id=1, source_target_pairs={{0,6},{2,0},{4,2},{6,4},{1,7},{3,1},{5,3},{7,5},{8,14},{10,8},{12,... | collective-permute-start | bytes 392 | tf_op jit(solution)/shard_map/ppermute | solution.py:438
  80.0 7.5 %collective-permute-start.17 = (f32[1,16]{1,0:T(1,128)S(1)}, f32[1,16]{1,0:T(1,128)S(1)}, u32[]{:S(2)}, u32[]{:S(2)}) collective-permute-start(f32[1,16]{1,0:T(1,128)S(1)} %get-tuple-element.67), channel_id=1, source_target_pairs={{0,1},{1,0},{2,3},{3,2},{4,5},{5,4},{6,7},{7,6},{8,9},{9,8},{10,11... | collective-permute-start | bytes 200 | tf_op jit(solution)/shard_map/ppermute | solution.py:443
